TPU v7x, 512 devices: a whole 4x8x8 slice. The times are simulated.
512 devices in a mesh: dp: 8 (over x, core), seq: 64 (over z, y).
Axes of the slice: x: 4, y: 8, z: 8, core: 2. Of those that a mesh axis runs over, the one named last changes fastest.
Arguments:
- queries: bfloat16 [8, 8192, 2048], P('dp', 'seq'), may hold values from -6 to 6
- keys: bfloat16 [8, 8192, 2048], P('dp', 'seq'), may hold values from -0.75 to 0.75
- values: bfloat16 [8, 8192, 2048], P('dp', 'seq'), may hold values from -6 to 6
- log_decay: float32 [8, 32, 8192], P('dp', None, 'seq'), may hold values from -0.7 to 0
- gain: float32 [2048], replicated, may hold values from 0.25 to 1.75
- d_out: bfloat16 [8, 8192, 2048], P('dp', 'seq'), may hold values from -12 to 12
Outputs:
- d_queries: bfloat16 [8, 8192, 2048], P('dp', 'seq')
- d_keys: bfloat16 [8, 8192, 2048], P('dp', 'seq')
- d_values: bfloat16 [8, 8192, 2048], P('dp', 'seq')
- d_log_decay: float32 [8, 32, 8192], P('dp', None, 'seq')
- d_gain: float32 [2048], replicated
All inputs are finite; a program needn't handle non-finite values.
Results may differ from a plain program's by a relative error of at most 0.001.
Values sent between devices are 32-bit elements; how exact they have to be, the bound alone decides.
No kernel may reach another device: no remote copies, remote signals or barrier semaphores. Data moves between devices by JAX's collectives and lax.ppermute only.
A program may use at most 192 MiB of HBM per device.

v0:
```python
import jax
import jax.numpy as jnp
from jax import lax
from jax.sharding import PartitionSpec as P

HIGH = lax.Precision.HIGHEST
EPSILON = 1e-06


def entering(part, axis, combine, identity, reverse):
    count = lax.axis_size(axis)
    place = lax.axis_index(axis)
    ahead = count - 1 - place if reverse else place
    gathered = jax.tree.map(lambda a: lax.all_gather(a, axis), part)
    state = jax.tree.map(lambda a, e: jnp.zeros_like(a) + jnp.asarray(e, a.dtype), part, identity)

    def one(hop, state):
        source = count - 1 - hop if reverse else hop
        return combine(
            state, jax.tree.map(lambda a: lax.dynamic_index_in_dim(a, source, 0, False), gathered)
        )

    return lax.fori_loop(0, ahead, one, state)


def decay_table(log_block):
    cumulative = jnp.cumsum(log_block, axis=1)
    spread = cumulative[:, :, None] - cumulative[:, None, :]
    length = log_block.shape[1]
    lower = jnp.arange(length)[:, None] >= jnp.arange(length)[None, :]
    table = jnp.where(lower[None], jnp.exp(jnp.minimum(spread, 0.0)), 0.0)
    return (cumulative, table)


def block_out(query, keys, values, log_block, start_state):
    cumulative, table = decay_table(log_block)
    scores = jnp.einsum("hdt,hds->hts", query, keys, precision=HIGH) * table
    inside = jnp.einsum("hts,hes->het", scores, values, precision=HIGH)
    carried = jnp.einsum("hdt,hde->het", query, start_state, precision=HIGH)
    return inside + jnp.exp(cumulative)[:, None, :] * carried


def block_end(keys, values, log_block, start_state):
    cumulative = jnp.cumsum(log_block, axis=1)
    total = cumulative[:, -1]
    weighted = keys * jnp.exp(total[:, None] - cumulative)[:, None, :]
    fresh = jnp.einsum("hds,hes->hde", weighted, values, precision=HIGH)
    return jnp.exp(total)[:, None, None] * start_state + fresh


def normalize(attended, gain):
    heads, width, length = attended.shape
    scale = jnp.sqrt(jnp.mean(attended * attended, axis=(0, 1)) + EPSILON)
    return attended / scale[None, None, :] * gain.reshape(heads, width, 1)


def chain(earlier, later):
    return (earlier[0] * later[0], later[0][:, None, None] * earlier[1] + later[1])


def shards(queries, keys, values, log_decay, gain, d_out):
    length = queries.shape[1]
    heads = log_decay.shape[1]
    width = queries.shape[2] // heads

    def split_heads(array):
        return jnp.transpose(array[0].reshape(length, heads, width), (1, 2, 0)).astype(jnp.float32)

    def merge_heads(array):
        return jnp.transpose(array.astype(jnp.bfloat16), (2, 0, 1)).reshape(length, heads * width)[
            None
        ]

    query_heads = split_heads(queries)
    key_heads = split_heads(keys)
    value_heads = split_heads(values)
    cotangent = split_heads(d_out)
    log_block = log_decay[0]
    decay_whole = jnp.exp(jnp.sum(log_block, axis=1))
    empty = jnp.zeros((heads, width, width), jnp.float32)
    fresh = block_end(key_heads, value_heads, log_block, empty)
    identity = (jnp.ones_like(decay_whole), empty)
    _, start_state = entering((decay_whole, fresh), "seq", chain, identity, False)

    def attend(query_in, key_in, value_in, log_in, state_in, gain_in):
        return normalize(block_out(query_in, key_in, value_in, log_in, state_in), gain_in)

    _, pull = jax.vjp(attend, query_heads, key_heads, value_heads, log_block, start_state, gain)
    d_query, d_key_inside, d_value_inside, d_log_inside, incoming, d_gain_local = pull(cotangent)
    _, end_grad = entering((decay_whole, incoming), "seq", chain, identity, True)

    def finish(key_in, value_in, log_in):
        return block_end(key_in, value_in, log_in, start_state)

    _, pull_end = jax.vjp(finish, key_heads, value_heads, log_block)
    d_key_carried, d_value_carried, d_log_carried = pull_end(end_grad)
    d_gain = lax.psum(d_gain_local, ("dp", "seq"))
    d_keys = merge_heads(d_key_inside + d_key_carried)
    d_values = merge_heads(d_value_inside + d_value_carried)
    d_log_decay = (d_log_inside + d_log_carried)[None]
    return (merge_heads(d_query), d_keys, d_values, d_log_decay, d_gain)


def solution(mesh):
    placed = (
        P("dp", "seq", None),
        P("dp", "seq", None),
        P("dp", "seq", None),
        P("dp", None, "seq"),
        P(),
        P("dp", "seq", None),
    )
    return jax.shard_map(
        shards,
        mesh=mesh,
        in_specs=placed,
        out_specs=(
            P("dp", "seq", None),
            P("dp", "seq", None),
            P("dp", "seq", None),
            P("dp", None, "seq"),
            P(),
        ),
        check_vma=False,
    )
```

profile of v0, /device:TPU:1, one launch (start us, length us, event | category | flops | bytes accessed | tf_op | source)
XLA Modules:
  0.0 1028.4 jit_solution(7607943299414100689)
XLA Ops:
  9.8 1.5 copy.66
  11.3 2.0 convolution_add_fusion
  15.6 131.7 %all-reduce.1 = f32[2048]{0:T(1024)S(1)} all-reduce(f32[2048]{0:T(1024)S(1)} %exponential_dynamic-update-slice_fusion), channel_id=2, replica_groups=mesh['dp'=8,'seq'=64] {'seq'}, use_global_device_ids=true, to_apply=%add.1 | all-reduce | flops 2048 | bytes 16384
  147.9 1.8 fusion.70
  149.8 265.6 %all-gather.6.cloned.1.call-done = f32[2048,64,64]{2,1,0:T(8,128)} async-done(((f32[32,64,64]{2,1,0:T(8,128)}), f32[2048,64,64]{2,1,0:T(8,128)}) %all-gather.6.cloned.1.call-update) | async-done | bytes 33554448 | tf_op jit(solution)/shard_map/all_gather | solution.py:14
  417.3 2.4 multiply_reduce_fusion.4
  420.4 1.8 multiply_reduce_fusion.2
  422.2 1.9 convolution_bitcast_fusion.1
  424.1 2.6 copy.70
  426.9 4.4 fusion.69
  431.3 2.5 fusion.14
  437.4 197.9 %psum.7 = f32[2048]{0:T(1024)} all-reduce(f32[2048]{0:T(1024)S(1)} %reshape.143), channel_id=1, replica_groups=mesh['dp'=8,'seq'=64] {'dp','seq'}, use_global_device_ids=true, to_apply=%region_17.18 | all-reduce | flops 2048 | bytes 16384 | tf_op jit(solution)/shard_map/psum | solution.py:97
  635.3 274.4 %all-gather.8.cloned.1.call-done = f32[2048,64,64]{2,1,0:T(8,128)} async-done(((f32[32,64,64]{2,1,0:T(8,128)}), f32[2048,64,64]{2,1,0:T(8,128)}) %all-gather.8.cloned.1.call-update) | async-done | bytes 33554448 | tf_op jit(solution)/shard_map/all_gather | solution.py:14
  909.8 94.3 %while.27 = (s32[]{:T(128)}, f32[32,64,64]{2,1,0:T(8,128)S(1)}, s32[]{:T(128)}, f32[64,32]{1,0:T(8,128)S(1)}, f32[64,32,64,64]{3,2,1,0:T(8,128)}, /*index=5*/s32[]{:T(128)}, s32[]{:T(128)}, s32[]{:T(128)}, s32[]{:T(128)}) while((s32[]{:T(128)}, f32[32,64,64]{2,1,0:T(8,128)S(1)}, s32[]{:T(128)}, f32[64,32]{1,0:T(8,128)S(1)}, ...), condition=%wide.region_7.8_spmd, body=%wide.region_6.7_spmd.sunk | while | flops 262150 | bytes 1573395 | solution.py:23
  909.8 1.4 bitcast_add_fusion.6
  911.3 1.4 bitcast_add_fusion.6
  912.8 1.4 bitcast_add_fusion.6
  914.3 1.4 bitcast_add_fusion.6
  915.8 1.4 bitcast_add_fusion.6
  917.3 1.4 bitcast_add_fusion.6
  918.8 1.4 bitcast_add_fusion.6
  920.3 1.4 bitcast_add_fusion.6
  921.8 1.4 bitcast_add_fusion.6
  923.3 1.4 bitcast_add_fusion.6
  924.8 1.4 bitcast_add_fusion.6
  926.3 1.4 bitcast_add_fusion.6
  927.8 1.4 bitcast_add_fusion.6
  929.3 1.4 bitcast_add_fusion.6
  930.8 1.4 bitcast_add_fusion.6
  932.3 1.4 bitcast_add_fusion.6
  933.8 1.4 bitcast_add_fusion.6
  935.2 1.4 bitcast_add_fusion.6
  936.7 1.4 bitcast_add_fusion.6
  938.2 1.4 bitcast_add_fusion.6
  939.7 1.4 bitcast_add_fusion.6
  941.2 1.4 bitcast_add_fusion.6
  942.7 1.4 bitcast_add_fusion.6
  944.2 1.4 bitcast_add_fusion.6
  945.7 1.4 bitcast_add_fusion.6
  947.2 1.4 bitcast_add_fusion.6
  948.7 1.4 bitcast_add_fusion.6
  950.2 1.4 bitcast_add_fusion.6
  951.7 1.4 bitcast_add_fusion.6
  953.2 1.4 bitcast_add_fusion.6
  954.7 1.4 bitcast_add_fusion.6
  956.2 1.4 bitcast_add_fusion.6
  957.7 1.4 bitcast_add_fusion.6
  959.2 1.4 bitcast_add_fusion.6
  960.7 1.4 bitcast_add_fusion.6
  962.2 1.4 bitcast_add_fusion.6
  963.7 1.4 bitcast_add_fusion.6
  965.2 1.4 bitcast_add_fusion.6
  966.7 1.4 bitcast_add_fusion.6
  968.2 1.4 bitcast_add_fusion.6
  969.7 1.4 bitcast_add_fusion.6
  971.2 1.4 bitcast_add_fusion.6
  972.7 1.4 bitcast_add_fusion.6
  974.2 1.4 bitcast_add_fusion.6
  987.6 1.4 bitcast_add_fusion.6
  1001.1 1.4 bitcast_add_fusion.6
  1005.3 1.7 fusion.41
  1007.0 2.8 fusion.40
  1010.1 4.4 fusion.37
  1015.5 3.2 fusion.33
  (159 shorter events, 41.7 us)
Async XLA Ops:
  7.2 408.2 %all-gather.6.cloned.1.call-start = ((), (), s32[]{:S(2)}) async-start(), calls=%async_computation | async-start | bytes 68157440 | tf_op jit(solution)/shard_map/all_gather | solution.py:14
  9.8 421.5 %copy-start = (bf16[1,128,2048]{1,2,0:T(8,128)(2,1)}, bf16[1,128,2048]{1,2,0:T(8,128)(2,1)S(1)}, u32[]{:S(2)}) copy-start(bf16[1,128,2048]{1,2,0:T(8,128)(2,1)S(1)} %copy.63) | copy-start | bytes 1572868
  9.8 3.6 copy-start.14
  9.8 137.5 %copy-start.13 = (bf16[1,128,2048]{2,1,0:T(8,128)(2,1)S(1)}, bf16[1,128,2048]{2,1,0:T(8,128)(2,1)}, u32[]{:S(2)}) copy-start(bf16[1,128,2048]{2,1,0:T(8,128)(2,1)} %param.10) | copy-start | bytes 1572868
  11.3 136.3 %copy-start.7 = (bf16[1,128,2048]{1,2,0:T(8,128)(2,1)}, bf16[1,128,2048]{1,2,0:T(8,128)(2,1)S(1)}, u32[]{:S(2)}) copy-start(bf16[1,128,2048]{1,2,0:T(8,128)(2,1)S(1)} %copy.66) | copy-start | bytes 1572868
  11.3 136.3 %copy-start.12 = (bf16[1,128,2048]{2,1,0:T(8,128)(2,1)S(1)}, bf16[1,128,2048]{2,1,0:T(8,128)(2,1)}, u32[]{:S(2)}) copy-start(bf16[1,128,2048]{2,1,0:T(8,128)(2,1)} %param.15) | copy-start | bytes 1572868
  13.3 134.6 %copy-start.15 = (f32[2048]{0:T(1024)S(1)}, f32[2048]{0:T(1024)}, u32[]{:S(2)}) copy-start(f32[2048]{0:T(1024)} %param.14) | copy-start | bytes 24580
  13.3 896.3 %all-gather.8.cloned.1.call-start = ((), (), s32[]{:S(2)}) async-start(), calls=%async_computation.1 | async-start | bytes 68157440 | tf_op jit(solution)/shard_map/all_gather | solution.py:14
  147.6 268.0 %copy-start.4 = (bf16[1,128,2048]{1,2,0:T(8,128)(2,1)}, bf16[1,128,2048]{1,2,0:T(8,128)(2,1)S(1)}, u32[]{:S(2)}) copy-start(bf16[1,128,2048]{1,2,0:T(8,128)(2,1)S(1)} %copy.68) | copy-start | bytes 1572868
  147.8 271.9 %copy-start.2 = (f32[1,128,2048]{1,2,0:T(8,128)}, f32[1,128,2048]{1,2,0:T(8,128)S(1)}, u32[]{:S(2)}) copy-start(f32[1,128,2048]{1,2,0:T(8,128)S(1)} %copy.67) | copy-start | bytes 3145732
  415.6 1.6 copy-start.3
  415.7 1.7 copy-start.8
  420.4 1.8 copy-start.5
  424.1 2.7 copy-start.9
  431.3 3.8 copy-start.16
  1004.1 1.0 copy-start.1
  1004.1 1.2 copy-start.10
  1010.1 5.4 copy-start.6
  1010.1 5.4 copy-start.11
Sparse Core Ops, SparseCore 0:
  13.4 401.8 all-gather.5
  426.9 482.7 all-gather.7
where the time goes:
time: 1030 us
  waiting for transfers between devices  540 us (52%)
  blocking collectives  330 us (32%)
  other arithmetic  98.3 us (10%)
  matrix products  29.4 us (3%)
  between operations  15.1 us (1%)
  local copies, waits for them, and re-layouts  13.3 us (1%)
    all_gather x2, waiting for transfers between devices, entering(): gathered = jax.tree.map(lambda a: lax.all_gather(a, axis), part)  540 us
    psum x1, blocking collectives, shards(): d_gain = lax.psum(d_gain_local, ('dp', 'seq'))  198 us
    unnamed x1, blocking collectives  132 us
    add x63, other arithmetic, chain(): later[0][:, None, None] * earlier[1] + later[1]  91.2 us
  transfers between devices with their start and end apart: 2, of which 2 were waited for; matrix products, arithmetic and copies ran while one was open for 1% of the time, Pallas kernels for 0%

commit v1 on v0

v1 whole, which is shorter than its diff:
```python
import jax
import jax.numpy as jnp
from jax import lax
from jax.experimental import pallas as pl
from jax.experimental.pallas import tpu as pltpu
from jax.sharding import PartitionSpec as P

HIGH = lax.Precision.HIGHEST
EPSILON = 1e-06
F32 = jnp.float32
BF16 = jnp.bfloat16
LANES = 128
NN = (((1,), (0,)), ((), ()))
NT = (((1,), (1,)), ((), ()))
TN = (((0,), (0,)), ((), ()))


def mm(a, b, dims=NN):
    return lax.dot_general(a, b, dims, preferred_element_type=F32)


def exact(a, b, dims=NN):
    return lax.dot_general(a, b, dims, precision=HIGH, preferred_element_type=F32)


def iota(shape, axis):
    return lax.broadcasted_iota(jnp.int32, shape, axis)


def halves(x):
    hi = x.astype(BF16)
    return hi, (x - hi.astype(F32)).astype(BF16)


def thirds(x):
    hi = x.astype(BF16)
    rest = x - hi.astype(F32)
    mid = rest.astype(BF16)
    return hi, mid, (rest - mid.astype(F32)).astype(BF16)


def expand(x, width, store):
    heads = x.shape[1]
    parts = thirds(x)
    for start in range(0, heads * width, 256):
        pick = (iota((heads, 256), 0) == (iota((heads, 256), 1) + start) // width).astype(F32).astype(BF16)
        store(start, sum(mm(part, pick) for part in parts))


def side(width):
    lane = iota((1, width), 1) & (LANES - 1)
    first = jnp.where(lane < LANES // 2, 1.0, 0.0).astype(F32)
    return first.astype(BF16), (1.0 - first).astype(BF16)


def stacked(x, m0, m1):
    return jnp.concatenate([x * m0, x * m1], axis=0)


def compact(full):
    lane = iota((LANES // 2, LANES), 1)
    return jnp.where(lane < LANES // 2, full[: LANES // 2], full[LANES // 2 :])


def sums(log, length):
    row, col = iota((length, length), 0), iota((length, length), 1)
    cumulative_t = exact((col <= row).astype(F32), log, NT)
    return cumulative_t, cumulative_t[length - 1 : length]


def fresh_kernel(k_ref, v_ref, log_ref, out_ref, weight):
    length, features = k_ref.shape
    pairs = features // LANES
    cumulative_t, total = sums(log_ref[...], length)

    def store(start, value):
        weight[:, start : start + 256] = value

    expand(
        jnp.concatenate(
            [jnp.exp(total - cumulative_t), jnp.broadcast_to(jnp.exp(total), (8, total.shape[1]))], 0
        ),
        64,
        store,
    )
    for p in range(pairs):
        lanes = slice(p * LANES, (p + 1) * LANES)
        k_t = k_ref[:, lanes].T
        hi, lo = halves(weight[:length, lanes] * v_ref[:, lanes].astype(F32))
        state = compact(mm(jnp.concatenate([k_t, k_t], 1), jnp.concatenate([hi, lo], 0)))
        decay = weight[length : length + 1, lanes]
        for i in range(4):
            j = 17 * (4 * p + i)
            out_ref[j : j + 16] = state[16 * i : 16 * i + 16]
            out_ref[j + 16 : j + 17] = decay


def scan_kernel(in_ref, out_ref, decay_ref):
    count = decay_ref.shape[0]
    state = jnp.zeros((16, LANES), F32)
    for m in range(count):
        out_ref[16 * m : 16 * m + 16] = state
        decay = in_ref[17 * m + 16 : 17 * m + 17]
        decay_ref[m : m + 1] = decay
        state = decay * state + in_ref[17 * m : 17 * m + 16]


def gain_kernel(in_ref, out_ref):
    count = in_ref.shape[0] // 17
    total = in_ref[16:17]
    for m in range(1, count):
        total = total + in_ref[17 * m + 16 : 17 * m + 17]
    out_ref[...] = jnp.broadcast_to(total[None], out_ref.shape)


def back_kernel(in_ref, decay_ref, gain_ref, out_ref):
    count = decay_ref.shape[0]
    gain = gain_ref[0, 0:1]
    for i in range(1, gain_ref.shape[0]):
        gain = gain + gain_ref[i, 0:1]
    state = jnp.zeros((16, LANES), F32)
    for m in range(count - 1, -1, -1):
        out_ref[17 * m : 17 * m + 16] = state
        out_ref[17 * m + 16 : 17 * m + 17] = gain
        state = decay_ref[m : m + 1] * state + in_ref[17 * m : 17 * m + 16]


def main_kernel(
    q_ref, k_ref, v_ref, g_ref, log_ref, gain_ref, state_ref,
    dq_ref, out_ref, dk_ref, dv_ref, z_ref,
    cum, cum_wide, grow, table, att, inner, gains,
):
    length, features = q_ref.shape
    heads = log_ref.shape[0]
    pairs = features // LANES
    log = log_ref[...]
    row, col = iota((length, length), 0), iota((length, length), 1)
    cum[...] = exact(log, (row <= col).astype(F32))
    cumulative_t, _ = sums(log, length)

    def store_wide(start, value):
        cum_wide[:, start : start + 256] = value

    def store_grow(start, value):
        grow[:, start : start + 256] = value

    expand(cumulative_t, LANES, store_wide)
    expand(jnp.exp(cumulative_t), 64, store_grow)
    m0, m1 = side(LANES)
    lower = row >= col
    upper = row <= col

    def block_diagonal(p):
        hi, lo = halves(state_ref[pl.ds(pl.multiple_of(p * 64, 64), 64), :])
        return stacked(hi, m0, m1), stacked(lo, m0, m1)

    def pair(p):
        return pl.ds(pl.multiple_of(p * LANES, LANES), LANES)

    def attend(p, carry):
        square, dot = carry
        lanes = pair(p)
        q, k, v = q_ref[:, lanes], k_ref[:, lanes], v_ref[:, lanes]
        score = mm(q, stacked(k, m0, m1), NT)
        decays = []
        for a in range(2):
            wide = cum_wide[:, pl.ds(pl.multiple_of((2 * p + a) * LANES, LANES), LANES)]
            spread = jnp.minimum(wide - cum[pl.ds(2 * p + a, 1), :], 0.0)
            decays.append(jnp.where(lower, jnp.exp(spread), 0.0))
        decay = jnp.concatenate(decays, 1)
        table[pl.ds(pl.multiple_of(p * LANES, LANES), LANES), :] = decay
        hi, lo = halves(score * decay)
        both = stacked(v, m0, m1)
        inside = mm(hi, both) + mm(lo, both)
        state_hi, state_lo = block_diagonal(p)
        carried = mm(jnp.concatenate([q, q], 1), jnp.concatenate([state_hi, state_lo], 0))
        attended = inside + grow[:, lanes] * carried
        att[:, lanes] = attended
        weighted = gain_ref[:, lanes] * g_ref[:, lanes].astype(F32)
        return square + attended * attended, dot + attended * weighted

    zero = jnp.zeros((length, LANES), F32)
    square, dot = lax.fori_loop(0, pairs, attend, (zero, zero))
    scale = jnp.sqrt(jnp.sum(square, 1, keepdims=True) / features + EPSILON)
    inverse = 1.0 / scale
    slope = jnp.sum(dot, 1, keepdims=True) * (inverse * inverse * inverse) / features
    z_ref[...] = jnp.zeros_like(z_ref)

    def pull(p, carry):
        lanes = pair(p)
        q, k, v = q_ref[:, lanes], k_ref[:, lanes], v_ref[:, lanes]
        attended = att[:, lanes]
        g = g_ref[:, lanes].astype(F32) * inverse
        gains[pl.ds(p, 1), :] = jnp.sum(g * attended, 0, keepdims=True)
        x = gain_ref[:, lanes] * g - attended * slope
        x_hi, x_lo = halves(x)
        y_hi, y_lo = halves(grow[:, lanes] * x)
        k2, q2, v2 = stacked(k, m0, m1), stacked(q, m0, m1), stacked(v, m0, m1)
        x2_hi, x2_lo = stacked(x_hi, m0, m1), stacked(x_lo, m0, m1)
        d_weight = mm(jnp.concatenate([x_hi, x_lo], 1), jnp.concatenate([v2, v2], 1), NT)
        hi, lo = halves(d_weight * table[pl.ds(pl.multiple_of(p * LANES, LANES), LANES), :])
        state_hi, state_lo = block_diagonal(p)
        dq = mm(hi, k2) + mm(lo, k2) + mm(y_hi, state_lo, NT)
        dq = dq + mm(jnp.concatenate([y_hi, y_lo], 1), jnp.concatenate([state_hi, state_hi], 1), NT)
        dq_ref[:, lanes] = dq.astype(BF16)
        decays = []
        for a in range(2):
            wide = cum_wide[:, pl.ds(pl.multiple_of((2 * p + a) * LANES, LANES), LANES)]
            spread = jnp.minimum(cum[pl.ds(2 * p + a, 1), :] - wide, 0.0)
            decays.append(jnp.where(upper, jnp.exp(spread), 0.0))
        decay = jnp.concatenate(decays, 1)
        hi, lo = halves(mm(k, q2, NT) * decay)
        dv_ref[:, lanes] = mm(hi, x2_hi) + mm(lo, x2_hi) + mm(hi, x2_lo)
        d_weight = mm(jnp.concatenate([v, v], 1), jnp.concatenate([x2_hi, x2_lo], 1), NT)
        hi, lo = halves(d_weight * decay)
        dk = mm(hi, q2) + mm(lo, q2)
        dk_ref[:, lanes] = dk
        q_t = q.T
        full = mm(jnp.concatenate([q_t, q_t], 1), jnp.concatenate([y_hi, y_lo], 0))
        inner[pl.ds(pl.multiple_of(p * 64, 64), 64), :] = compact(full)
        hi, lo = halves(q.astype(F32) * dq - k.astype(F32) * dk)
        z_ref[...] += mm(picker(heads, p), jnp.concatenate([hi, lo], 1), NT)
        return carry

    lax.fori_loop(0, pairs, pull, 0)
    for j in range(4 * pairs):
        out_ref[17 * j : 17 * j + 16] = inner[16 * j : 16 * j + 16]
        out_ref[17 * j + 16 : 17 * j + 17] = gains[j // 4 : j // 4 + 1]


def picker(heads, p):
    lane = iota((heads, 2 * LANES), 1) & (LANES - 1)
    head = 2 * p + lane // 64
    return (iota((heads, 2 * LANES), 0) == head).astype(F32).astype(BF16)


def last_kernel(
    k_ref, v_ref, log_ref, state_ref, dk_in, dv_in, z_ref, in_ref,
    dk_ref, dv_ref, log_out, gain_out,
    weight, inner, kept,
):
    length, features = k_ref.shape
    heads = log_ref.shape[0]
    pairs = features // LANES
    log = log_ref[...]
    cumulative_t, total = sums(log, length)

    def store(start, value):
        weight[:, start : start + 256] = value

    expand(jnp.exp(total - cumulative_t), 64, store)
    for j in range(4 * pairs):
        inner[16 * j : 16 * j + 16] = in_ref[17 * j : 17 * j + 16]
    for p in range(pairs):
        gain_out[p : p + 1] = in_ref[17 * 4 * p + 16 : 17 * 4 * p + 17]
    m0, m1 = side(LANES)
    lane = iota((1, LANES), 1)

    def finish(p, u):
        lanes = pl.ds(pl.multiple_of(p * LANES, LANES), LANES)
        rows = pl.ds(pl.multiple_of(p * 64, 64), 64)
        k, v = k_ref[:, lanes], v_ref[:, lanes]
        grad = inner[rows, :]
        hi, lo = halves(grad)
        hi, lo = stacked(hi, m0, m1), stacked(lo, m0, m1)
        w = weight[:, lanes]
        dk = w * mm(jnp.concatenate([v, v], 1), jnp.concatenate([hi, lo], 1), NT)
        dv = w * mm(jnp.concatenate([k, k], 1), jnp.concatenate([hi, lo], 0))
        dk_ref[:, lanes] = (dk_in[:, lanes] + dk).astype(BF16)
        dv_ref[:, lanes] = (dv_in[:, lanes] + dv).astype(BF16)
        part = jnp.sum(grad * state_ref[rows, :], 0, keepdims=True)
        kept[pl.ds(2 * p, 1), :] = jnp.where(lane < 64, part, 0.0)
        kept[pl.ds(2 * p + 1, 1), :] = jnp.where(lane < 64, 0.0, part)
        hi, lo = halves(k.astype(F32) * dk)
        return u + mm(picker(heads, p), jnp.concatenate([hi, lo], 1), NT)

    u = lax.fori_loop(0, pairs, finish, jnp.zeros((heads, length), F32))
    row, col = iota((length, length), 0), iota((length, length), 1)
    whole = jnp.exp(jnp.sum(log, 1, keepdims=True)) * jnp.sum(kept[...], 1, keepdims=True)
    log_out[...] = (
        exact(z_ref[...], (row >= col).astype(F32)) + exact(u, (row < col).astype(F32)) + whole
    )


def call(kernel, outs, scratch, flops, *args):
    vmem = pl.BlockSpec(memory_space=pltpu.VMEM)
    outs = [jax.ShapeDtypeStruct(shape, dtype) for shape, dtype in outs]
    size = sum(a.size * a.dtype.itemsize for a in [*args, *outs])
    return pl.pallas_call(
        kernel,
        out_shape=outs,
        in_specs=[vmem] * len(args),
        out_specs=[vmem] * len(outs),
        scratch_shapes=[pltpu.VMEM(shape, dtype) for shape, dtype in scratch],
        cost_estimate=pl.CostEstimate(flops=flops, bytes_accessed=size, transcendentals=0),
        compiler_params=pltpu.CompilerParams(vmem_limit_bytes=48 << 20),
    )(*args)


def exchange(array, axis):
    count = lax.axis_size(axis)
    rows, lanes = array.shape
    pieces = array.reshape(count, 1, rows // count * lanes)
    return lax.all_to_all(pieces, axis, 0, 0, tiled=True).reshape(rows, lanes)


def shards(queries, keys, values, log_decay, gain, d_out):
    length, features = queries.shape[1:]
    heads = log_decay.shape[1]
    pairs = features // LANES
    count = lax.axis_size("seq")
    assert features == 32 * count and features == 64 * heads and length == LANES
    q, k, v, g, log = queries[0], keys[0], values[0], d_out[0], log_decay[0]
    wide = (length, features)
    sent = (17 * count, LANES)
    states = (16 * count, LANES)

    (fresh,) = call(fresh_kernel, [(sent, F32)], [((length + 8, features), F32)], 1 << 27, k, v, log)
    begun, decays = call(
        scan_kernel, [(states, F32), ((count, LANES), F32)], [], 1 << 20, exchange(fresh, "seq")
    )
    start = exchange(begun, "seq")
    d_queries, incoming, dk, dv, z = call(
        main_kernel,
        [(wide, BF16), (sent, F32), (wide, F32), (wide, F32), ((heads, length), F32)],
        [
            ((heads, length), F32),
            ((length, heads * LANES), F32),
            (wide, F32),
            ((features, 2 * LANES), F32),
            (wide, F32),
            (states, F32),
            ((pairs, LANES), F32),
        ],
        1 << 30,
        q, k, v, g, log, gain[None], start,
    )
    arrived = exchange(incoming, "seq")
    groups = lax.axis_size("dp")
    (partial,) = call(gain_kernel, [((groups, 8, LANES), F32)], [], 1 << 10, arrived)
    partial = lax.all_to_all(partial, "dp", 0, 0, tiled=True)
    (ended,) = call(back_kernel, [(sent, F32)], [], 1 << 20, arrived, decays, partial)
    d_keys, d_values, d_log, d_gain = call(
        last_kernel,
        [(wide, BF16), (wide, BF16), ((heads, length), F32), ((pairs, LANES), F32)],
        [(wide, F32), (states, F32), ((heads, LANES), F32)],
        1 << 28,
        k, v, log, start, dk, dv, z, exchange(ended, "seq"),
    )
    return d_queries[None], d_keys[None], d_values[None], d_log[None], d_gain.reshape(features)


def solution(mesh):
    tokens, decays = P("dp", "seq", None), P("dp", None, "seq")
    return jax.shard_map(
        shards,
        mesh=mesh,
        in_specs=(tokens, tokens, tokens, decays, P(), tokens),
        out_specs=(tokens, tokens, tokens, decays, P()),
        check_vma=False,
    )
```

time: 1030 us -> 155 us (0.15)
  waiting for transfers between devices: 540 us -> 0 us
  blocking collectives: 330 us -> 117 us
  other arithmetic: 98.3 us -> 0 us
  Pallas kernels: 0 us -> 31.4 us
  matrix products: 29.4 us -> 0 us
  between operations: 15.1 us -> 0.7 us
  local copies, waits for them, and re-layouts: 13.3 us -> 2.82 us
    all_gather x2 -> x0, waiting for transfers between devices: 540 us -> none  [entering(): gathered = jax.tree.map(lambda a: lax.all_gather(a, axis), part)]
    psum x1 -> x0, blocking collectives: 198 us -> none  [shards(): d_gain = lax.psum(d_gain_local, ('dp', 'seq'))]
    unnamed x1 -> x0, blocking collectives: 132 us -> none
    all_to_all x0 -> x5, blocking collectives: none -> 117 us  [the longest x4 103 us: exchange(): return lax.all_to_all(pieces, axis, 0, 0, tiled=True).reshape(rows, lanes)]
    add x64 -> x0, other arithmetic: 91.8 us -> none  [the longest x63 91.2 us: chain(): later[0][:, None, None] * earlier[1] + later[1]]
    pallas_call x0 -> x6, Pallas kernels: none -> 31.4 us  [call(): pl.pallas_call(kernel, out_shape=outs, in_specs=[vmem] * len(args), out_s...]
    dot_general x12 -> x0, matrix products: 29.4 us -> none  [the longest x3 11.1 us: block_out(): inside = jnp.einsum('hts,hes->het', scores, values, precision=HIGH)]
  transfers between devices with their start and end apart: 2 -> 0, of which waited for: 2 -> 0; matrix products, arithmetic and copies ran while one was open for 1% -> 0% of each run, Pallas kernels for 0% -> 0%
where the time goes in v1:
time: 155 us; the launch traced here: 152 us
  blocking collectives  117 us (75%)
  Pallas kernels  31.4 us (20%)
  local copies, waits for them, and re-layouts  2.82 us (2%)
    all_to_all x4, blocking collectives, exchange(): return lax.all_to_all(pieces, axis, 0, 0, tiled=True).reshape(rows, lanes)  103 us
    pallas_call x6, Pallas kernels, call(): pl.pallas_call(kernel, out_shape=outs, in_specs=[vmem] * len(args), out_s...  31.4 us
    all_to_all x1, blocking collectives, shards(): partial = lax.all_to_all(partial, 'dp', 0, 0, tiled=True)  13.8 us

profile of v1, /device:TPU:1, one launch (start us, length us, event | category | flops | bytes accessed | tf_op | source)
XLA Modules:
  0.0 152.2 jit_solution(2001854955467394138)
XLA Ops:
  0.6 0.0 copy-start
  0.6 1.0 copy-done
  1.7 0.0 copy-start.2
  1.7 1.0 copy-done.2
  2.7 0.0 copy-start.4
  2.7 0.7 copy-done.4
  3.4 1.2 shard_map.101
  4.6 0.0 copy-start.7
  4.6 34.6 %all_to_all.25 = f32[64,1,2176]{2,1,0:T(1,128)S(1)} all-to-all(f32[64,1,2176]{2,1,0:T(1,128)S(1)} %bitcast.23), channel_id=1, replica_groups=mesh['dp'=8,'seq'=64] {'seq'}, dimensions={0} | all-to-all | bytes 1114112 | tf_op jit(solution)/shard_map/all_to_all | solution.py:304
  39.2 0.0 copy-start.5
  39.2 0.0 copy-start.6
  39.2 0.0 copy-start.8
  39.2 0.1 shard_map.102
  39.4 0.0 copy-start.1
  39.4 0.0 copy-start.3
  39.4 23.3 %all_to_all.26 = f32[64,1,2048]{2,1,0:T(1,128)S(1)} all-to-all(f32[64,1,2048]{2,1,0:T(1,128)S(1)} %bitcast.34), channel_id=1, replica_groups=mesh['dp'=8,'seq'=64] {'seq'}, dimensions={0} | all-to-all | bytes 1048576 | tf_op jit(solution)/shard_map/all_to_all | solution.py:304
  62.7 0.0 copy-done.7
  62.7 0.0 copy-done.5
  62.7 0.0 copy-done.6
  62.7 0.0 copy-done.8
  62.7 0.0 copy-done.1
  62.8 0.0 copy-done.3
  62.8 23.1 %shard_map.103 = (bf16[128,2048]{1,0:T(8,128)(2,1)}, f32[1088,128]{1,0:T(8,128)S(1)}, f32[128,2048]{1,0:T(8,128)S(1)}, f32[128,2048]{1,0:T(8,128)S(1)}, f32[32,128]{1,0:T(8,128)S(1)}) custom-call(bf16[128,2048]{1,0:T(8,128)(2,1)S(1)} %bitcast.38, bf16[128,2048]{1,0:T(8,128)(2,1)S(1)} %bitcast.26, bf16[128,2048]{1,0:T(8,128)(2,1)S(1)} %bitcast.29, ...), custom_call_target="tpu_custom_call" | custom-call | flops 1073741824 | bytes 5840896 | tf_op jit(solution)/shard_map/pallas_call | solution.py:289
  85.9 23.2 %all_to_all.27 = f32[64,1,2176]{2,1,0:T(1,128)S(1)} all-to-all(f32[64,1,2176]{2,1,0:T(1,128)S(1)} %bitcast.33), channel_id=1, replica_groups=mesh['dp'=8,'seq'=64] {'seq'}, dimensions={0} | all-to-all | bytes 1114112 | tf_op jit(solution)/shard_map/all_to_all | solution.py:304
  109.1 0.1 shard_map.104
  109.2 13.8 %all_to_all.28.gain_ref = f32[8,8,128]{2,1,0:T(8,128)S(1)} all-to-all(f32[8,8,128]{2,1,0:T(8,128)S(1)} %shard_map.104), channel_id=1, replica_groups=mesh['dp'=8,'seq'=64] {'dp'}, dimensions={0} | all-to-all | bytes 65536 | tf_op jit(solution)/shard_map/all_to_all | solution.py:341
  123.0 0.1 shard_map.105
  123.2 22.3 %all_to_all.29 = f32[64,1,2176]{2,1,0:T(1,128)S(1)} all-to-all(f32[64,1,2176]{2,1,0:T(1,128)S(1)} %bitcast.22), channel_id=1, replica_groups=mesh['dp'=8,'seq'=64] {'seq'}, dimensions={0} | all-to-all | bytes 1114112 | tf_op jit(solution)/shard_map/all_to_all | solution.py:304
  145.4 6.8 %shard_map.106 = (bf16[128,2048]{1,0:T(8,128)(2,1)}, bf16[128,2048]{1,0:T(8,128)(2,1)}, f32[32,128]{1,0:T(8,128)}, f32[16,128]{1,0:T(8,128)}) custom-call(bf16[128,2048]{1,0:T(8,128)(2,1)S(1)} %bitcast.27, bf16[128,2048]{1,0:T(8,128)(2,1)S(1)} %bitcast.30, f32[32,128]{1,0:T(8,128)S(1)} %bitcast.37, f32[1024,128]{1,0:T(8,128)S(1)} %bitcast.32, ...), custom_call_target="tpu_custom_call" | custom-call | flops 268435456 | bytes 5332992 | tf_op jit(solution)/shard_map/pallas_call | solution.py:289
Async XLA Ops:
  0.6 1.0 copy-start
  1.7 1.0 copy-start.2
  2.7 0.7 copy-start.4
  4.6 58.1 %copy-start.7 = (bf16[1,128,2048]{2,1,0:T(8,128)(2,1)S(1)}, bf16[1,128,2048]{2,1,0:T(8,128)(2,1)}, u32[]{:S(2)}) copy-start(bf16[1,128,2048]{2,1,0:T(8,128)(2,1)} %param.11) | copy-start | bytes 1572868
  39.2 23.5 %copy-start.5 = (f32[1,32,128]{2,1,0:T(8,128)S(1)}, f32[1,32,128]{2,1,0:T(8,128)}, u32[]{:S(2)}) copy-start(f32[1,32,128]{2,1,0:T(8,128)} %param.9) | copy-start | bytes 49156
  39.2 23.5 %copy-start.6 = (bf16[1,128,2048]{2,1,0:T(8,128)(2,1)S(1)}, bf16[1,128,2048]{2,1,0:T(8,128)(2,1)}, u32[]{:S(2)}) copy-start(bf16[1,128,2048]{2,1,0:T(8,128)(2,1)} %param.6) | copy-start | bytes 1572868
  39.2 23.5 %copy-start.8 = (f32[2048]{0:T(1024)S(1)}, f32[2048]{0:T(1024)}, u32[]{:S(2)}) copy-start(f32[2048]{0:T(1024)} %param.10) | copy-start | bytes 24580
  39.4 23.4 %copy-start.1 = (bf16[1,128,2048]{2,1,0:T(8,128)(2,1)S(1)}, bf16[1,128,2048]{2,1,0:T(8,128)(2,1)}, u32[]{:S(2)}) copy-start(bf16[1,128,2048]{2,1,0:T(8,128)(2,1)} %param.7) | copy-start | bytes 1572868
  39.4 23.4 %copy-start.3 = (bf16[1,128,2048]{2,1,0:T(8,128)(2,1)S(1)}, bf16[1,128,2048]{2,1,0:T(8,128)(2,1)}, u32[]{:S(2)}) copy-start(bf16[1,128,2048]{2,1,0:T(8,128)(2,1)} %param.8) | copy-start | bytes 1572868

commit v2 on v1

v2 whole, which is shorter than its diff:
```python
import math

import jax
import jax.numpy as jnp
from jax import lax
from jax.experimental import pallas as pl
from jax.experimental.pallas import tpu as pltpu
from jax.sharding import PartitionSpec as P

HIGH = lax.Precision.HIGHEST
EPSILON = 1e-06
F32 = jnp.float32
BF16 = jnp.bfloat16
LANES = 128
NN = (((1,), (0,)), ((), ()))
NT = (((1,), (1,)), ((), ()))
TN = (((0,), (0,)), ((), ()))


def mm(a, b, dims=NN):
    return lax.dot_general(a, b, dims, preferred_element_type=F32)


def exact(a, b, dims=NN):
    return lax.dot_general(a, b, dims, precision=HIGH, preferred_element_type=F32)


def iota(shape, axis):
    return lax.broadcasted_iota(jnp.int32, shape, axis)


def halves(x):
    hi = x.astype(BF16)
    return hi, (x - hi.astype(F32)).astype(BF16)


def thirds(x):
    hi = x.astype(BF16)
    rest = x - hi.astype(F32)
    mid = rest.astype(BF16)
    return hi, mid, (rest - mid.astype(F32)).astype(BF16)


def expand(x, width, store):
    heads = x.shape[1]
    parts = thirds(x)
    for start in range(0, heads * width, 256):
        pick = (iota((heads, 256), 0) == (iota((heads, 256), 1) + start) // width).astype(F32).astype(BF16)
        store(start, sum(mm(part, pick) for part in parts))


def side(width):
    lane = iota((1, width), 1) & (LANES - 1)
    first = jnp.where(lane < LANES // 2, 1.0, 0.0).astype(F32)
    return first.astype(BF16), (1.0 - first).astype(BF16)


def stacked(x, m0, m1):
    return jnp.concatenate([x * m0, x * m1], axis=0)


def compact(full):
    lane = iota((LANES // 2, LANES), 1)
    return jnp.where(lane < LANES // 2, full[: LANES // 2], full[LANES // 2 :])


def sums(log, length):
    row, col = iota((length, length), 0), iota((length, length), 1)
    cumulative_t = exact((col <= row).astype(F32), log, NT)
    return cumulative_t, cumulative_t[length - 1 : length]


def pair(p):
    return slice(p * LANES, (p + 1) * LANES)


def block_diagonal(state, m0, m1):
    hi, lo = halves(state)
    return stacked(hi, m0, m1), stacked(lo, m0, m1)


def decay_pair(wide_ref, cum_ref, p, keep, sign):
    parts = []
    for h in (2 * p, 2 * p + 1):
        spread = wide_ref[:, pair(h)] - cum_ref[h : h + 1, :]
        parts.append(jnp.where(keep, jnp.exp(jnp.minimum(sign * spread, 0.0)), 0.0))
    return jnp.concatenate(parts, 1)


def writer(ref):
    def store(start, value):
        ref[:, start : start + 256] = value

    return store


def send_state(out_ref, p, state, row):
    for i in range(4):
        j = 17 * (4 * p + i)
        out_ref[j : j + 16] = state[16 * i : 16 * i + 16]
        out_ref[j + 16 : j + 17] = row


def fresh_kernel(ready, emit, log_ref, k_ref, v_ref, out_ref, weight):
    length, features = k_ref.shape
    ready("log")
    cumulative_t, total = sums(log_ref[...], length)
    ends = jnp.broadcast_to(jnp.exp(total), (8, total.shape[1]))
    expand(jnp.concatenate([jnp.exp(total - cumulative_t), ends], 0), 64, writer(weight))
    for p in range(features // LANES):
        if p % 4 == 0:
            ready(p // 4)
        lanes = pair(p)
        k_t = k_ref[:, lanes].T
        hi, lo = halves(weight[:length, lanes] * v_ref[:, lanes].astype(F32))
        state = compact(mm(jnp.concatenate([k_t, k_t], 1), jnp.concatenate([hi, lo], 0)))
        send_state(out_ref, p, state, weight[length : length + 1, lanes])
        if p % 4 == 3:
            emit(p // 4)


def scan_kernel(in_ref, out_ref, decay_ref):
    count = decay_ref.shape[0]
    state = jnp.zeros((16, LANES), F32)
    for m in range(count):
        out_ref[16 * m : 16 * m + 16] = state
        decay = in_ref[17 * m + 16 : 17 * m + 17]
        decay_ref[m : m + 1] = decay
        state = decay * state + in_ref[17 * m : 17 * m + 16]


def back_kernel(in_ref, decay_ref, out_ref):
    count = decay_ref.shape[0]
    gain = in_ref[16:17]
    for m in range(1, count):
        gain = gain + in_ref[17 * m + 16 : 17 * m + 17]
    state = jnp.zeros((16, LANES), F32)
    for m in range(count - 1, -1, -1):
        out_ref[17 * m : 17 * m + 16] = state
        out_ref[17 * m + 16 : 17 * m + 17] = gain
        state = decay_ref[m : m + 1] * state + in_ref[17 * m : 17 * m + 16]


def gain_kernel(in_ref, out_ref, rows, sems):
    pairs = rows.shape[0]

    def copy(p):
        row = pl.ds(17 * 4 * p + 16, 1)
        return pltpu.make_async_copy(in_ref.at[row, :], rows.at[pl.ds(p, 1), :], sems.at[p])

    for p in range(pairs):
        copy(p).start()
    for p in range(pairs):
        copy(p).wait()
    out_ref[...] = jnp.broadcast_to(rows[...][None], out_ref.shape)


def gain_sum_kernel(in_ref, out_ref):
    total = in_ref[0]
    for d in range(1, in_ref.shape[0]):
        total = total + in_ref[d]
    out_ref[...] = total


def inside_kernel(
    ready, emit, log_ref, q_ref, k_ref, v_ref, cum_ref, wide_ref, grow_ref, weight_ref, inside_ref
):
    length, features = q_ref.shape
    ready("log")
    log = log_ref[...]
    row, col = iota((length, length), 0), iota((length, length), 1)
    cum_ref[...] = exact(log, (row <= col).astype(F32))
    cumulative_t, total = sums(log, length)
    expand(cumulative_t, LANES, writer(wide_ref))
    expand(jnp.exp(cumulative_t), 64, writer(grow_ref))
    expand(jnp.exp(total - cumulative_t), 64, writer(weight_ref))
    m0, m1 = side(LANES)
    for p in range(features // LANES):
        if p % 4 == 0:
            ready(p // 4)
        lanes = pair(p)
        score = mm(q_ref[:, lanes], stacked(k_ref[:, lanes], m0, m1), NT)
        hi, lo = halves(score * decay_pair(wide_ref, cum_ref, p, row >= col, 1.0))
        both = stacked(v_ref[:, lanes], m0, m1)
        inside_ref[:, lanes] = mm(hi, both) + mm(lo, both)
        if p % 4 == 3:
            emit(p // 4)


def middle_kernel(
    ready, emit, gain_ref, q_ref, g_ref, state_ref, grow_ref, inside_ref, out_ref, x_ref, att
):
    length, features = q_ref.shape
    pairs = features // LANES
    m0, m1 = side(LANES)
    square = dot = jnp.zeros((length, LANES), F32)
    ready("gain")
    for p in range(pairs):
        if p % 4 == 0:
            ready(p // 4)
        lanes = pair(p)
        q = q_ref[:, lanes]
        state_hi, state_lo = block_diagonal(state_ref[64 * p : 64 * p + 64], m0, m1)
        carried = mm(jnp.concatenate([q, q], 1), jnp.concatenate([state_hi, state_lo], 0))
        attended = inside_ref[:, lanes] + grow_ref[:, lanes] * carried
        att[:, lanes] = attended
        square = square + attended * attended
        dot = dot + attended * (gain_ref[:, lanes] * g_ref[:, lanes].astype(F32))
    scale = jnp.sqrt(jnp.sum(square, 1, keepdims=True) / features + EPSILON)
    inverse = 1.0 / scale
    slope = jnp.sum(dot, 1, keepdims=True) * (inverse * inverse * inverse) / features
    for p in range(pairs):
        lanes = pair(p)
        attended = att[:, lanes]
        g = g_ref[:, lanes].astype(F32) * inverse
        gain_row = jnp.sum(g * attended, 0, keepdims=True)
        x = gain_ref[:, lanes] * g - attended * slope
        x_ref[:, lanes] = x
        hi, lo = halves(grow_ref[:, lanes] * x)
        q_t = q_ref[:, lanes].T
        state = compact(mm(jnp.concatenate([q_t, q_t], 1), jnp.concatenate([hi, lo], 0)))
        send_state(out_ref, p, state, gain_row)
        if p % 4 == 3:
            emit(p // 4)


def local_kernel(
    ready, emit, cum_ref, q_ref, k_ref, v_ref, wide_ref, grow_ref, x_ref, state_ref,
    z_ref, dq_ref, dk_ref, dv_ref,
):
    length, features = q_ref.shape
    heads = cum_ref.shape[0]
    m0, m1 = side(LANES)
    row, col = iota((length, length), 0), iota((length, length), 1)
    z = jnp.zeros((heads, length), F32)
    ready("cum")
    for p in range(features // LANES):
        if p % 4 == 0:
            ready(p // 4)
        lanes = pair(p)
        q, k, v, x = q_ref[:, lanes], k_ref[:, lanes], v_ref[:, lanes], x_ref[:, lanes]
        x_hi, x_lo = halves(x)
        y_hi, y_lo = halves(grow_ref[:, lanes] * x)
        k2, q2, v2 = stacked(k, m0, m1), stacked(q, m0, m1), stacked(v, m0, m1)
        x2_hi, x2_lo = stacked(x_hi, m0, m1), stacked(x_lo, m0, m1)
        d_weight = mm(jnp.concatenate([x_hi, x_lo], 1), jnp.concatenate([v2, v2], 1), NT)
        hi, lo = halves(d_weight * decay_pair(wide_ref, cum_ref, p, row >= col, 1.0))
        state_hi, state_lo = block_diagonal(state_ref[64 * p : 64 * p + 64], m0, m1)
        dq = mm(hi, k2) + mm(lo, k2) + mm(y_hi, state_lo, NT)
        dq = dq + mm(jnp.concatenate([y_hi, y_lo], 1), jnp.concatenate([state_hi, state_hi], 1), NT)
        dq_ref[:, lanes] = dq.astype(BF16)
        decay = decay_pair(wide_ref, cum_ref, p, row <= col, -1.0)
        hi, lo = halves(mm(k, q2, NT) * decay)
        dv_ref[:, lanes] = mm(hi, x2_hi) + mm(lo, x2_hi) + mm(hi, x2_lo)
        d_weight = mm(jnp.concatenate([v, v], 1), jnp.concatenate([x2_hi, x2_lo], 1), NT)
        hi, lo = halves(d_weight * decay)
        dk = mm(hi, q2) + mm(lo, q2)
        dk_ref[:, lanes] = dk
        hi, lo = halves(q.astype(F32) * dq - k.astype(F32) * dk)
        z = z + mm(picker(heads, p), jnp.concatenate([hi, lo], 1), NT)
        if p % 4 == 3:
            emit(p // 4)
    z_ref[...] = z


def picker(heads, p):
    lane = iota((heads, 2 * LANES), 1) & (LANES - 1)
    head = 2 * p + lane // 64
    return (iota((heads, 2 * LANES), 0) == head).astype(F32).astype(BF16)


def last_kernel(
    ready, emit, log_ref, z_ref, in_ref, k_ref, v_ref, weight_ref, state_ref, dk_in, dv_in,
    log_out, dk_ref, dv_ref, kept,
):
    length, features = k_ref.shape
    heads = log_ref.shape[0]
    m0, m1 = side(LANES)
    lane = iota((1, LANES), 1)
    u = jnp.zeros((heads, length), F32)
    ready("log")
    ready("z")
    for p in range(features // LANES):
        if p % 4 == 0:
            ready(p // 4)
        lanes = pair(p)
        k, v, w = k_ref[:, lanes], v_ref[:, lanes], weight_ref[:, lanes]
        j = 17 * 4 * p
        grad = jnp.concatenate([in_ref[j + 17 * i : j + 17 * i + 16] for i in range(4)], 0)
        hi, lo = block_diagonal(grad, m0, m1)
        dk = w * mm(jnp.concatenate([v, v], 1), jnp.concatenate([hi, lo], 1), NT)
        dv = w * mm(jnp.concatenate([k, k], 1), jnp.concatenate([hi, lo], 0))
        dk_ref[:, lanes] = (dk_in[:, lanes] + dk).astype(BF16)
        dv_ref[:, lanes] = (dv_in[:, lanes] + dv).astype(BF16)
        part = jnp.sum(grad * state_ref[64 * p : 64 * p + 64], 0, keepdims=True)
        kept[2 * p : 2 * p + 1] = jnp.where(lane < 64, part, 0.0)
        kept[2 * p + 1 : 2 * p + 2] = jnp.where(lane < 64, 0.0, part)
        hi, lo = halves(k.astype(F32) * dk)
        u = u + mm(picker(heads, p), jnp.concatenate([hi, lo], 1), NT)
        if p % 4 == 3:
            emit(p // 4)
    row, col = iota((length, length), 0), iota((length, length), 1)
    whole = jnp.exp(jnp.sum(log_ref[...], 1, keepdims=True)) * jnp.sum(kept[...], 1, keepdims=True)
    log_out[...] = (
        exact(z_ref[...], (row >= col).astype(F32)) + exact(u, (row < col).astype(F32)) + whole
    )


def call(kernel, outs, flops, *args):
    vmem = pl.BlockSpec(memory_space=pltpu.VMEM)
    outs = [jax.ShapeDtypeStruct(shape, dtype) for shape, dtype in outs]
    size = sum(a.size * a.dtype.itemsize for a in [*args, *outs])
    return pl.pallas_call(
        kernel,
        out_shape=outs,
        in_specs=[vmem] * len(args),
        out_specs=[vmem] * len(outs),
        cost_estimate=pl.CostEstimate(flops=flops, bytes_accessed=size, transcendentals=0),
        compiler_params=pltpu.CompilerParams(vmem_limit_bytes=4 << 20),
    )(*args)


def staged(kernel, flops, limit, ins, outs, scratch=()):
    in_shapes = [(a.shape, a.dtype) for a in ins.values()]
    out_shapes = list(outs.values())
    names = [*ins, *outs]
    shapes = in_shapes + out_shapes
    small = [shape[0] <= 32 for shape, _ in shapes]
    count = len(shapes)

    def body(*refs):
        far, near = refs[:count], refs[count : 2 * count]
        sems, own = refs[2 * count], refs[2 * count + 1 :]

        def copy(i, c):
            rows, lanes = shapes[i][0]
            if small[i]:
                a, b = far[i], near[i]
            elif lanes == LANES:
                part = pl.ds(c * (rows // 4), rows // 4)
                a, b = far[i].at[part, :], near[i].at[part, :]
            else:
                part = pl.ds(c * (lanes // 4), lanes // 4)
                a, b = far[i].at[:, part], near[i].at[:, part]
            if i >= len(ins):
                a, b = b, a
            return pltpu.make_async_copy(a, b, sems.at[i, c])

        sent = range(len(ins), count)
        for i in range(len(ins)):
            if small[i]:
                copy(i, 0).start()
        for c in range(4):
            for i in range(len(ins)):
                if not small[i]:
                    copy(i, c).start()

        def ready(c):
            for i in range(len(ins)):
                if small[i] and names[i] == c:
                    copy(i, 0).wait()
                if not small[i] and c in range(4):
                    copy(i, c).wait()

        def emit(c):
            for i in sent:
                if not small[i]:
                    copy(i, c).start()

        kernel(ready, emit, *near, *own)
        for i in sent:
            if small[i]:
                copy(i, 0).start()
        for i in sent:
            for c in range(1 if small[i] else 4):
                copy(i, c).wait()

    hbm = pl.BlockSpec(memory_space=pltpu.HBM)
    results = [jax.ShapeDtypeStruct(shape, dtype) for shape, dtype in out_shapes]
    size = sum(math.prod(shape) * jnp.dtype(dtype).itemsize for shape, dtype in shapes)
    return pl.pallas_call(
        body,
        out_shape=results,
        in_specs=[hbm] * len(ins),
        out_specs=[hbm] * len(outs),
        scratch_shapes=[
            *(pltpu.VMEM(shape, dtype) for shape, dtype in shapes),
            pltpu.SemaphoreType.DMA((count, 4)),
            *(pltpu.VMEM(shape, dtype) for shape, dtype in scratch),
        ],
        cost_estimate=pl.CostEstimate(flops=flops, bytes_accessed=size, transcendentals=0),
        compiler_params=pltpu.CompilerParams(vmem_limit_bytes=limit << 20),
    )(*ins.values())


def exchange(array, axis):
    count = lax.axis_size(axis)
    rows, lanes = array.shape
    pieces = array.reshape(count, 1, rows // count * lanes)
    return lax.all_to_all(pieces, axis, 0, 0, tiled=True).reshape(rows, lanes)


def shards(queries, keys, values, log_decay, gain, d_out):
    length, features = queries.shape[1:]
    heads = log_decay.shape[1]
    pairs = features // LANES
    count = lax.axis_size("seq")
    assert features == 32 * count and features == 64 * heads and length == LANES
    q, k, v, g, log = queries[0], keys[0], values[0], d_out[0], log_decay[0]
    wide = ((length, features), F32)
    half = ((length, features), BF16)
    small = ((heads, length), F32)
    sent = ((17 * count, LANES), F32)

    (fresh,) = staged(
        fresh_kernel, 1 << 27, 60, dict(log=log, k=k, v=v), dict(out=sent),
        [((length + 8, features), F32)],
    )
    arrived = exchange(fresh, "seq")
    cum, spread, grow, weight, inside = staged(
        inside_kernel, 1 << 30, 60, dict(log=log, q=q, k=k, v=v),
        dict(cum=small, spread=((length, heads * LANES), F32), grow=wide, weight=wide, inside=wide),
    )
    arrived, inside = lax.optimization_barrier((arrived, inside))
    begun, decays = call(
        scan_kernel, [((16 * count, LANES), F32), ((count, LANES), F32)], 1 << 20, arrived
    )
    start = exchange(begun, "seq")
    incoming, x = staged(
        middle_kernel, 1 << 28, 60,
        dict(gain=gain[None], q=q, g=g, state=start, grow=grow, inside=inside),
        dict(out=sent, x=wide), [wide],
    )
    returned = exchange(incoming, "seq")
    z, d_queries, dk, dv = staged(
        local_kernel, 1 << 31, 60,
        dict(cum=cum, q=q, k=k, v=v, spread=spread, grow=grow, x=x, state=start),
        dict(z=small, dq=half, dk=wide, dv=wide),
    )
    returned, dk = lax.optimization_barrier((returned, dk))
    (ended,) = call(back_kernel, [sent], 1 << 20, returned, decays)
    ended = exchange(ended, "seq")
    shares = jax.ShapeDtypeStruct((lax.axis_size("dp"), pairs, LANES), F32)
    share = pl.pallas_call(
        gain_kernel,
        out_shape=shares,
        in_specs=[pl.BlockSpec(memory_space=pltpu.HBM)],
        out_specs=pl.BlockSpec(memory_space=pltpu.VMEM),
        scratch_shapes=[pltpu.VMEM((pairs, LANES), F32), pltpu.SemaphoreType.DMA((pairs,))],
        compiler_params=pltpu.CompilerParams(vmem_limit_bytes=60 << 20),
    )(ended)
    share = lax.all_to_all(share, "dp", 0, 0, tiled=True)
    (d_gain,) = call(gain_sum_kernel, [((pairs, LANES), F32)], 1 << 10, share)
    d_log, d_keys, d_values = staged(
        last_kernel, 1 << 28, 60,
        {"log": log, "z": z, "in": ended, "k": k, "v": v, "w": weight, "s": start, "dk": dk, "dv": dv},
        dict(log=small, dk=half, dv=half), [((heads, LANES), F32)],
    )
    return d_queries[None], d_keys[None], d_values[None], d_log[None], d_gain.reshape(features)


def solution(mesh):
    tokens, decays = P("dp", "seq", None), P("dp", None, "seq")
    return jax.shard_map(
        shards,
        mesh=mesh,
        in_specs=(tokens, tokens, tokens, decays, P(), tokens),
        out_specs=(tokens, tokens, tokens, decays, P()),
        check_vma=False,
    )
```

time: 155 us -> 132 us (0.85); the launches traced: 152 us -> 131 us
  blocking collectives: 117 us -> 47.1 us
  starting transfers between devices: 0 us -> 34.4 us
  waiting for transfers between devices: 0 us -> 14.3 us
  Pallas kernels: 31.4 us -> 34.3 us
  local copies, waits for them, and re-layouts: 2.82 us -> 0 us
    all_to_all x4 -> x2, blocking collectives: 103 us -> 47.1 us  [exchange(): return lax.all_to_all(pieces, axis, 0, 0, tiled=True).reshape(rows, lanes)]
    all_to_all x0 -> x3, starting transfers between devices: none -> 34.4 us  [the longest x2 24.6 us: exchange(): return lax.all_to_all(pieces, axis, 0, 0, tiled=True).reshape(rows, lanes)]
    pallas_call x0 -> x6, Pallas kernels: none -> 33.4 us  [the longest x5 31.9 us: staged(): pl.pallas_call(body, out_shape=results, in_specs=[hbm] * len(ins), out_sp...]
    pallas_call x6 -> x3, Pallas kernels: 31.4 us -> 0.89 us  [call(): pl.pallas_call(kernel, out_shape=outs, in_specs=[vmem] * len(args), out_s...]
    all_to_all x0 -> x3, waiting for transfers between devices: none -> 14.3 us  [the longest x2 14.3 us: exchange(): return lax.all_to_all(pieces, axis, 0, 0, tiled=True).reshape(rows, lanes)]
    all_to_all x1 -> x0, blocking collectives: 13.8 us -> none  [shards(): partial = lax.all_to_all(partial, 'dp', 0, 0, tiled=True)]
    unnamed x18 -> x0, local copies, waits for them, and re-layouts: 2.82 us -> none
  transfers between devices with their start and end apart: 0 -> 3, of which waited for: 0 -> 3; matrix products, arithmetic and copies ran while one was open for 0% -> 0% of each run, Pallas kernels for 0% -> 18%
where the time goes in v2:
time: 132 us; the launch traced here: 131 us
  blocking collectives  47.1 us (36%)
  starting transfers between devices  34.4 us (26%)
  Pallas kernels  34.3 us (26%)
  waiting for transfers between devices  14.3 us (11%)
    all_to_all x2, blocking collectives, exchange(): return lax.all_to_all(pieces, axis, 0, 0, tiled=True).reshape(rows, lanes)  47.1 us
    pallas_call x5, Pallas kernels, staged(): pl.pallas_call(body, out_shape=results, in_specs=[hbm] * len(ins), out_sp...  31.9 us
    all_to_all x2, starting transfers between devices, exchange(): return lax.all_to_all(pieces, axis, 0, 0, tiled=True).reshape(rows, lanes)  24.6 us
    all_to_all x2, waiting for transfers between devices, exchange(): return lax.all_to_all(pieces, axis, 0, 0, tiled=True).reshape(rows, lanes)  14.3 us
    all_to_all x1, starting transfers between devices, shards(): share = lax.all_to_all(share, 'dp', 0, 0, tiled=True)  9.81 us
  transfers between devices with their start and end apart: 3, of which 3 were waited for; matrix products, arithmetic and copies ran while one was open for 0% of the time, Pallas kernels for 18%

profile of v2, /device:TPU:1, one launch (start us, length us, event | category | flops | bytes accessed | tf_op | source)
XLA Modules:
  0.0 130.8 jit_solution(1041899761197523525)
XLA Ops:
  0.6 3.5 %shard_map.102 = f32[1088,128]{1,0:T(8,128)} custom-call(f32[32,128]{1,0:T(8,128)} %bitcast.42, bf16[128,2048]{1,0:T(8,128)(2,1)} %bitcast.29, bf16[128,2048]{1,0:T(8,128)(2,1)} %bitcast.33), custom_call_target="tpu_custom_call" | custom-call | flops 134217728 | bytes 1622016 | tf_op jit(solution)/shard_map/pallas_call | solution.py:381
  4.1 17.1 %all-to-all-start = ((f32[64,1,2176]{2,1,0:T(1,128)}), f32[64,1,2176]{2,1,0:T(1,128)S(1)}, u32[]{:S(2)}, u32[]{:S(2)}) async-start(f32[64,1,2176]{2,1,0:T(1,128)} %bitcast.28), calls=%async_computation | async-start | bytes 1114112 | tf_op jit(solution)/shard_map/all_to_all | solution.py:400
  21.3 7.1 %shard_map.101 = (f32[32,128]{1,0:T(8,128)}, f32[128,4096]{1,0:T(8,128)}, f32[128,2048]{1,0:T(8,128)}, f32[128,2048]{1,0:T(8,128)}, f32[128,2048]{1,0:T(8,128)}) custom-call(f32[32,128]{1,0:T(8,128)} %bitcast.43, bf16[128,2048]{1,0:T(8,128)(2,1)} %bitcast.39, bf16[128,2048]{1,0:T(8,128)(2,1)} %bitcast.30, bf16[128,2048]{1,0:T(8,128)(2,1)} %bitcast.34), custom_call_target="tpu_custom_call" | custom-call | flops 1073741824 | bytes 6848512 | tf_op jit(solution)/shard_map/pallas_call | solution.py:381
  28.4 10.4 %all-to-all-done = f32[64,1,2176]{2,1,0:T(1,128)S(1)} async-done(((f32[64,1,2176]{2,1,0:T(1,128)}), f32[64,1,2176]{2,1,0:T(1,128)S(1)}, u32[]{:S(2)}, u32[]{:S(2)}) %all-to-all-start) | async-done | bytes 557088 | tf_op jit(solution)/shard_map/all_to_all | solution.py:400
  38.8 0.1 shard_map.103
  38.9 23.3 %all_to_all.25 = f32[64,1,2048]{2,1,0:T(1,128)} all-to-all(f32[64,1,2048]{2,1,0:T(1,128)S(1)} %bitcast.22), channel_id=1, replica_groups=mesh['dp'=8,'seq'=64] {'seq'}, dimensions={0} | all-to-all | bytes 1048576 | tf_op jit(solution)/shard_map/all_to_all | solution.py:400
  62.2 4.4 %shard_map.104 = (f32[1088,128]{1,0:T(8,128)}, f32[128,2048]{1,0:T(8,128)}) custom-call(f32[1,2048]{1,0:T(1,128)} %bitcast.45, bf16[128,2048]{1,0:T(8,128)(2,1)} %bitcast.40, bf16[128,2048]{1,0:T(8,128)(2,1)} %bitcast.38, f32[1024,128]{1,0:T(8,128)} %bitcast.25, f32[128,2048]{1,0:T(8,128)} %get-tuple-element.27.refs_4_.refs_5_, ...), custom_call_target="tpu_custom_call" | custom-call | flops 268435456 | bytes 5283840 | tf_op jit(solution)/shard_map/pallas_call | solution.py:381
  66.7 7.5 %all-to-all-start.2 = ((f32[64,1,2176]{2,1,0:T(1,128)}), f32[64,1,2176]{2,1,0:T(1,128)S(1)}, u32[]{:S(2)}, u32[]{:S(2)}) async-start(f32[64,1,2176]{2,1,0:T(1,128)} %bitcast.37), calls=%async_computation.2 | async-start | bytes 1114112 | tf_op jit(solution)/shard_map/all_to_all | solution.py:400
  74.2 12.1 %shard_map.105 = (f32[32,128]{1,0:T(8,128)}, bf16[128,2048]{1,0:T(8,128)(2,1)}, f32[128,2048]{1,0:T(8,128)}, f32[128,2048]{1,0:T(8,128)}) custom-call(f32[32,128]{1,0:T(8,128)} %get-tuple-element.25.refs_0_, bf16[128,2048]{1,0:T(8,128)(2,1)} %bitcast.41, bf16[128,2048]{1,0:T(8,128)(2,1)} %bitcast.31, bf16[128,2048]{1,0:T(8,128)(2,1)} %bitcast.35, ...), custom_call_target="tpu_custom_call" | custom-call | flops 2147483648 | bytes 8945664 | tf_op jit(solution)/shard_map/pallas_call | solution.py:381
  86.3 3.8 %all-to-all-done.2 = f32[64,1,2176]{2,1,0:T(1,128)S(1)} async-done(((f32[64,1,2176]{2,1,0:T(1,128)}), f32[64,1,2176]{2,1,0:T(1,128)S(1)}, u32[]{:S(2)}, u32[]{:S(2)}) %all-to-all-start.2) | async-done | bytes 557088 | tf_op jit(solution)/shard_map/all_to_all | solution.py:400
  90.1 0.1 shard_map.106
  90.3 23.8 %all_to_all.26 = f32[64,1,2176]{2,1,0:T(1,128)} all-to-all(f32[64,1,2176]{2,1,0:T(1,128)S(1)} %bitcast.21), channel_id=1, replica_groups=mesh['dp'=8,'seq'=64] {'seq'}, dimensions={0} | all-to-all | bytes 1114112 | tf_op jit(solution)/shard_map/all_to_all | solution.py:400
  114.1 1.5 %shard_map.108 = f32[8,16,128]{2,1,0:T(8,128)} custom-call(f32[1088,128]{1,0:T(8,128)} %bitcast.23), custom_call_target="tpu_custom_call" | custom-call | tf_op jit(solution)/shard_map/pallas_call | solution.py:444
  115.6 9.8 %all-to-all-start.4 = ((f32[8,16,128]{2,1,0:T(8,128)}), f32[8,16,128]{2,1,0:T(8,128)S(1)}, u32[]{:S(2)}, u32[]{:S(2)}) async-start(f32[8,16,128]{2,1,0:T(8,128)} %shard_map.108), calls=%async_computation.4 | async-start | bytes 131072 | tf_op jit(solution)/shard_map/all_to_all | solution.py:452
  125.4 4.8 %shard_map.107 = (f32[32,128]{1,0:T(8,128)}, bf16[128,2048]{1,0:T(8,128)(2,1)}, bf16[128,2048]{1,0:T(8,128)(2,1)}) custom-call(f32[32,128]{1,0:T(8,128)} %bitcast.44, f32[32,128]{1,0:T(8,128)} %get-tuple-element.34.refs_1_, f32[1088,128]{1,0:T(8,128)} %bitcast.24, bf16[128,2048]{1,0:T(8,128)(2,1)} %bitcast.32, bf16[128,2048]{1,0:T(8,128)(2,1)} %bitcast.36, ...), custom_call_target="tpu_custom_call" | custom-call | flops 268435456 | bytes 6373376 | tf_op jit(solution)/shard_map/pallas_call | solution.py:381
  130.2 0.1 all-to-all-done.4.in_ref
  130.2 0.6 shard_map.109
Async XLA Ops:
  4.1 34.7 %all-to-all-start = ((f32[64,1,2176]{2,1,0:T(1,128)}), f32[64,1,2176]{2,1,0:T(1,128)S(1)}, u32[]{:S(2)}, u32[]{:S(2)}) async-start(f32[64,1,2176]{2,1,0:T(1,128)} %bitcast.28), calls=%async_computation | async-start | bytes 1114112 | tf_op jit(solution)/shard_map/all_to_all | solution.py:400
  66.7 23.5 %all-to-all-start.2 = ((f32[64,1,2176]{2,1,0:T(1,128)}), f32[64,1,2176]{2,1,0:T(1,128)S(1)}, u32[]{:S(2)}, u32[]{:S(2)}) async-start(f32[64,1,2176]{2,1,0:T(1,128)} %bitcast.37), calls=%async_computation.2 | async-start | bytes 1114112 | tf_op jit(solution)/shard_map/all_to_all | solution.py:400
  115.6 14.7 %all-to-all-start.4 = ((f32[8,16,128]{2,1,0:T(8,128)}), f32[8,16,128]{2,1,0:T(8,128)S(1)}, u32[]{:S(2)}, u32[]{:S(2)}) async-start(f32[8,16,128]{2,1,0:T(8,128)} %shard_map.108), calls=%async_computation.4 | async-start | bytes 131072 | tf_op jit(solution)/shard_map/all_to_all | solution.py:452

commit v3 on v2

--- a/solution.py
+++ b/solution.py
@@ -12,6 +12,7 @@
 F32 = jnp.float32
 BF16 = jnp.bfloat16
 LANES = 128
+PAIRS = 16
 NN = (((1,), (0,)), ((), ()))
 NT = (((1,), (1,)), ((), ()))
 TN = (((0,), (0,)), ((), ()))
@@ -34,19 +35,9 @@
     return hi, (x - hi.astype(F32)).astype(BF16)
 
 
-def thirds(x):
-    hi = x.astype(BF16)
-    rest = x - hi.astype(F32)
-    mid = rest.astype(BF16)
-    return hi, mid, (rest - mid.astype(F32)).astype(BF16)
-
-
-def expand(x, width, store):
-    heads = x.shape[1]
-    parts = thirds(x)
-    for start in range(0, heads * width, 256):
-        pick = (iota((heads, 256), 0) == (iota((heads, 256), 1) + start) // width).astype(F32).astype(BF16)
-        store(start, sum(mm(part, pick) for part in parts))
+def columns(x, p):
+    lane = iota((1, LANES), 1)
+    return jnp.where(lane < LANES // 2, x[:, 2 * p : 2 * p + 1], x[:, 2 * p + 1 : 2 * p + 2])
 
 
 def side(width):
@@ -79,19 +70,16 @@
     return stacked(hi, m0, m1), stacked(lo, m0, m1)
 
 
-def decay_pair(wide_ref, cum_ref, p, keep, sign):
+def carry(q, state_hi, state_lo):
+    return mm(jnp.concatenate([q, q], 1), jnp.concatenate([state_hi, state_lo], 0))
+
+
+def decay_pair(cum_t, cum_ref, p, keep, sign):
     parts = []
     for h in (2 * p, 2 * p + 1):
-        spread = wide_ref[:, pair(h)] - cum_ref[h : h + 1, :]
+        spread = cum_t[:, h : h + 1] - cum_ref[h : h + 1, :]
         parts.append(jnp.where(keep, jnp.exp(jnp.minimum(sign * spread, 0.0)), 0.0))
     return jnp.concatenate(parts, 1)
-
-
-def writer(ref):
-    def store(start, value):
-        ref[:, start : start + 256] = value
-
-    return store
 
 
 def send_state(out_ref, p, state, row):
@@ -101,22 +89,19 @@
         out_ref[j + 16 : j + 17] = row
 
 
-def fresh_kernel(ready, emit, log_ref, k_ref, v_ref, out_ref, weight):
+def fresh_kernel(ready, emit, log_ref, k_ref, v_ref, out_ref):
     length, features = k_ref.shape
     ready("log")
     cumulative_t, total = sums(log_ref[...], length)
-    ends = jnp.broadcast_to(jnp.exp(total), (8, total.shape[1]))
-    expand(jnp.concatenate([jnp.exp(total - cumulative_t), ends], 0), 64, writer(weight))
+    weight, ends = jnp.exp(total - cumulative_t), jnp.exp(total)
     for p in range(features // LANES):
-        if p % 4 == 0:
-            ready(p // 4)
+        ready(p)
         lanes = pair(p)
         k_t = k_ref[:, lanes].T
-        hi, lo = halves(weight[:length, lanes] * v_ref[:, lanes].astype(F32))
+        hi, lo = halves(columns(weight, p) * v_ref[:, lanes].astype(F32))
         state = compact(mm(jnp.concatenate([k_t, k_t], 1), jnp.concatenate([hi, lo], 0)))
-        send_state(out_ref, p, state, weight[length : length + 1, lanes])
-        if p % 4 == 3:
-            emit(p // 4)
+        send_state(out_ref, p, state, columns(ends, p))
+        emit(p)
 
 
 def scan_kernel(in_ref, out_ref, decay_ref):
@@ -163,7 +148,7 @@
 
 
 def inside_kernel(
-    ready, emit, log_ref, q_ref, k_ref, v_ref, cum_ref, wide_ref, grow_ref, weight_ref, inside_ref
+    ready, emit, log_ref, q_ref, k_ref, v_ref, cum_ref, cum_t_ref, grow_ref, weight_ref, inside_ref
 ):
     length, features = q_ref.shape
     ready("log")
@@ -171,61 +156,58 @@
     row, col = iota((length, length), 0), iota((length, length), 1)
     cum_ref[...] = exact(log, (row <= col).astype(F32))
     cumulative_t, total = sums(log, length)
-    expand(cumulative_t, LANES, writer(wide_ref))
-    expand(jnp.exp(cumulative_t), 64, writer(grow_ref))
-    expand(jnp.exp(total - cumulative_t), 64, writer(weight_ref))
+    cum_t_ref[...] = cumulative_t
+    grow_ref[...] = jnp.exp(cumulative_t)
+    weight_ref[...] = jnp.exp(total - cumulative_t)
     m0, m1 = side(LANES)
     for p in range(features // LANES):
-        if p % 4 == 0:
-            ready(p // 4)
+        ready(p)
         lanes = pair(p)
         score = mm(q_ref[:, lanes], stacked(k_ref[:, lanes], m0, m1), NT)
-        hi, lo = halves(score * decay_pair(wide_ref, cum_ref, p, row >= col, 1.0))
+        hi, lo = halves(score * decay_pair(cumulative_t, cum_ref, p, row >= col, 1.0))
         both = stacked(v_ref[:, lanes], m0, m1)
         inside_ref[:, lanes] = mm(hi, both) + mm(lo, both)
-        if p % 4 == 3:
-            emit(p // 4)
+        emit(p)
 
 
 def middle_kernel(
-    ready, emit, gain_ref, q_ref, g_ref, state_ref, grow_ref, inside_ref, out_ref, x_ref, att
+    ready, emit, gain_ref, grow_ref, q_ref, g_ref, state_ref, inside_ref, stats_ref, out_ref, att
 ):
     length, features = q_ref.shape
     pairs = features // LANES
     m0, m1 = side(LANES)
     square = dot = jnp.zeros((length, LANES), F32)
     ready("gain")
+    ready("grow")
+    grow = grow_ref[...]
     for p in range(pairs):
-        if p % 4 == 0:
-            ready(p // 4)
-        lanes = pair(p)
-        q = q_ref[:, lanes]
-        state_hi, state_lo = block_diagonal(state_ref[64 * p : 64 * p + 64], m0, m1)
-        carried = mm(jnp.concatenate([q, q], 1), jnp.concatenate([state_hi, state_lo], 0))
-        attended = inside_ref[:, lanes] + grow_ref[:, lanes] * carried
+        ready(p)
+        lanes = pair(p)
+        carried = carry(q_ref[:, lanes], *block_diagonal(state_ref[64 * p : 64 * p + 64], m0, m1))
+        attended = inside_ref[:, lanes] + columns(grow, p) * carried
         att[:, lanes] = attended
         square = square + attended * attended
         dot = dot + attended * (gain_ref[:, lanes] * g_ref[:, lanes].astype(F32))
     scale = jnp.sqrt(jnp.sum(square, 1, keepdims=True) / features + EPSILON)
     inverse = 1.0 / scale
     slope = jnp.sum(dot, 1, keepdims=True) * (inverse * inverse * inverse) / features
+    stats_ref[...] = jnp.where(iota(stats_ref.shape, 1) == 0, inverse, slope)
     for p in range(pairs):
         lanes = pair(p)
         attended = att[:, lanes]
         g = g_ref[:, lanes].astype(F32) * inverse
         gain_row = jnp.sum(g * attended, 0, keepdims=True)
         x = gain_ref[:, lanes] * g - attended * slope
-        x_ref[:, lanes] = x
-        hi, lo = halves(grow_ref[:, lanes] * x)
+        hi, lo = halves(columns(grow, p) * x)
         q_t = q_ref[:, lanes].T
         state = compact(mm(jnp.concatenate([q_t, q_t], 1), jnp.concatenate([hi, lo], 0)))
         send_state(out_ref, p, state, gain_row)
-        if p % 4 == 3:
-            emit(p // 4)
+        emit(p)
 
 
 def local_kernel(
-    ready, emit, cum_ref, q_ref, k_ref, v_ref, wide_ref, grow_ref, x_ref, state_ref,
+    ready, emit, cum_ref, cum_t_ref, grow_ref, stats_ref, gain_ref,
+    q_ref, k_ref, v_ref, g_ref, state_ref, inside_ref,
     z_ref, dq_ref, dk_ref, dv_ref,
 ):
     length, features = q_ref.shape
@@ -233,23 +215,29 @@
     m0, m1 = side(LANES)
     row, col = iota((length, length), 0), iota((length, length), 1)
     z = jnp.zeros((heads, length), F32)
-    ready("cum")
+    for name in ("cum", "cum_t", "grow", "stats", "gain"):
+        ready(name)
+    cum_t, grow = cum_t_ref[...], grow_ref[...]
+    inverse, slope = stats_ref[:, 0:1], stats_ref[:, 1:2]
     for p in range(features // LANES):
-        if p % 4 == 0:
-            ready(p // 4)
-        lanes = pair(p)
-        q, k, v, x = q_ref[:, lanes], k_ref[:, lanes], v_ref[:, lanes], x_ref[:, lanes]
+        ready(p)
+        lanes = pair(p)
+        q, k, v = q_ref[:, lanes], k_ref[:, lanes], v_ref[:, lanes]
+        state_hi, state_lo = block_diagonal(state_ref[64 * p : 64 * p + 64], m0, m1)
+        growth = columns(grow, p)
+        attended = inside_ref[:, lanes] + growth * carry(q, state_hi, state_lo)
+        g = g_ref[:, lanes].astype(F32) * inverse
+        x = gain_ref[:, lanes] * g - attended * slope
         x_hi, x_lo = halves(x)
-        y_hi, y_lo = halves(grow_ref[:, lanes] * x)
+        y_hi, y_lo = halves(growth * x)
         k2, q2, v2 = stacked(k, m0, m1), stacked(q, m0, m1), stacked(v, m0, m1)
         x2_hi, x2_lo = stacked(x_hi, m0, m1), stacked(x_lo, m0, m1)
         d_weight = mm(jnp.concatenate([x_hi, x_lo], 1), jnp.concatenate([v2, v2], 1), NT)
-        hi, lo = halves(d_weight * decay_pair(wide_ref, cum_ref, p, row >= col, 1.0))
-        state_hi, state_lo = block_diagonal(state_ref[64 * p : 64 * p + 64], m0, m1)
+        hi, lo = halves(d_weight * decay_pair(cum_t, cum_ref, p, row >= col, 1.0))
         dq = mm(hi, k2) + mm(lo, k2) + mm(y_hi, state_lo, NT)
         dq = dq + mm(jnp.concatenate([y_hi, y_lo], 1), jnp.concatenate([state_hi, state_hi], 1), NT)
         dq_ref[:, lanes] = dq.astype(BF16)
-        decay = decay_pair(wide_ref, cum_ref, p, row <= col, -1.0)
+        decay = decay_pair(cum_t, cum_ref, p, row <= col, -1.0)
         hi, lo = halves(mm(k, q2, NT) * decay)
         dv_ref[:, lanes] = mm(hi, x2_hi) + mm(lo, x2_hi) + mm(hi, x2_lo)
         d_weight = mm(jnp.concatenate([v, v], 1), jnp.concatenate([x2_hi, x2_lo], 1), NT)
@@ -258,9 +246,8 @@
         dk_ref[:, lanes] = dk
         hi, lo = halves(q.astype(F32) * dq - k.astype(F32) * dk)
         z = z + mm(picker(heads, p), jnp.concatenate([hi, lo], 1), NT)
-        if p % 4 == 3:
-            emit(p // 4)
-    z_ref[...] = z
+        emit(p)
+    z_ref[...] = exact(z, (row >= col).astype(F32))
 
 
 def picker(heads, p):
@@ -270,7 +257,7 @@
 
 
 def last_kernel(
-    ready, emit, log_ref, z_ref, in_ref, k_ref, v_ref, weight_ref, state_ref, dk_in, dv_in,
+    ready, emit, log_ref, z_ref, weight_ref, in_ref, k_ref, v_ref, state_ref, dk_in, dv_in,
     log_out, dk_ref, dv_ref, kept,
 ):
     length, features = k_ref.shape
@@ -280,11 +267,12 @@
     u = jnp.zeros((heads, length), F32)
     ready("log")
     ready("z")
+    ready("w")
+    weight = weight_ref[...]
     for p in range(features // LANES):
-        if p % 4 == 0:
-            ready(p // 4)
-        lanes = pair(p)
-        k, v, w = k_ref[:, lanes], v_ref[:, lanes], weight_ref[:, lanes]
+        ready(p)
+        lanes = pair(p)
+        k, v, w = k_ref[:, lanes], v_ref[:, lanes], columns(weight, p)
         j = 17 * 4 * p
         grad = jnp.concatenate([in_ref[j + 17 * i : j + 17 * i + 16] for i in range(4)], 0)
         hi, lo = block_diagonal(grad, m0, m1)
@@ -297,13 +285,10 @@
         kept[2 * p + 1 : 2 * p + 2] = jnp.where(lane < 64, 0.0, part)
         hi, lo = halves(k.astype(F32) * dk)
         u = u + mm(picker(heads, p), jnp.concatenate([hi, lo], 1), NT)
-        if p % 4 == 3:
-            emit(p // 4)
+        emit(p)
     row, col = iota((length, length), 0), iota((length, length), 1)
     whole = jnp.exp(jnp.sum(log_ref[...], 1, keepdims=True)) * jnp.sum(kept[...], 1, keepdims=True)
-    log_out[...] = (
-        exact(z_ref[...], (row >= col).astype(F32)) + exact(u, (row < col).astype(F32)) + whole
-    )
+    log_out[...] = z_ref[...] + exact(u, (row < col).astype(F32)) + whole
 
 
 def call(kernel, outs, flops, *args):
@@ -320,12 +305,12 @@
     )(*args)
 
 
-def staged(kernel, flops, limit, ins, outs, scratch=()):
+def staged(kernel, flops, limit, pieces, ins, outs, scratch=()):
     in_shapes = [(a.shape, a.dtype) for a in ins.values()]
     out_shapes = list(outs.values())
     names = [*ins, *outs]
     shapes = in_shapes + out_shapes
-    small = [shape[0] <= 32 for shape, _ in shapes]
+    small = [math.prod(shape) <= 4096 for shape, _ in shapes]
     count = len(shapes)
 
     def body(*refs):
@@ -334,45 +319,48 @@
 
         def copy(i, c):
             rows, lanes = shapes[i][0]
+            cut = pieces[i >= len(ins)]
             if small[i]:
                 a, b = far[i], near[i]
             elif lanes == LANES:
-                part = pl.ds(c * (rows // 4), rows // 4)
+                part = pl.ds(c * (rows // cut), rows // cut)
                 a, b = far[i].at[part, :], near[i].at[part, :]
             else:
-                part = pl.ds(c * (lanes // 4), lanes // 4)
+                part = pl.ds(c * (lanes // cut), lanes // cut)
                 a, b = far[i].at[:, part], near[i].at[:, part]
             if i >= len(ins):
                 a, b = b, a
             return pltpu.make_async_copy(a, b, sems.at[i, c])
 
+        came = range(len(ins))
         sent = range(len(ins), count)
-        for i in range(len(ins)):
+        steps = [PAIRS // cut for cut in pieces]
+        for i in came:
             if small[i]:
                 copy(i, 0).start()
-        for c in range(4):
-            for i in range(len(ins)):
+        for c in range(pieces[0]):
+            for i in came:
                 if not small[i]:
                     copy(i, c).start()
 
-        def ready(c):
-            for i in range(len(ins)):
-                if small[i] and names[i] == c:
+        def ready(p):
+            for i in came:
+                if small[i] and names[i] == p:
                     copy(i, 0).wait()
-                if not small[i] and c in range(4):
-                    copy(i, c).wait()
-
-        def emit(c):
+                if not small[i] and p in range(0, PAIRS, steps[0]):
+                    copy(i, p // steps[0]).wait()
+
+        def emit(p):
             for i in sent:
-                if not small[i]:
-                    copy(i, c).start()
+                if not small[i] and p % steps[1] == steps[1] - 1:
+                    copy(i, p // steps[1]).start()
 
         kernel(ready, emit, *near, *own)
         for i in sent:
             if small[i]:
                 copy(i, 0).start()
         for i in sent:
-            for c in range(1 if small[i] else 4):
+            for c in range(1 if small[i] else pieces[1]):
                 copy(i, c).wait()
 
     hbm = pl.BlockSpec(memory_space=pltpu.HBM)
@@ -385,7 +373,7 @@
         out_specs=[hbm] * len(outs),
         scratch_shapes=[
             *(pltpu.VMEM(shape, dtype) for shape, dtype in shapes),
-            pltpu.SemaphoreType.DMA((count, 4)),
+            pltpu.SemaphoreType.DMA((count, max(pieces))),
             *(pltpu.VMEM(shape, dtype) for shape, dtype in scratch),
         ],
         cost_estimate=pl.CostEstimate(flops=flops, bytes_accessed=size, transcendentals=0),
@@ -405,36 +393,37 @@
     heads = log_decay.shape[1]
     pairs = features // LANES
     count = lax.axis_size("seq")
-    assert features == 32 * count and features == 64 * heads and length == LANES
+    assert features == 32 * count and features == 64 * heads and length == LANES and pairs == PAIRS
     q, k, v, g, log = queries[0], keys[0], values[0], d_out[0], log_decay[0]
     wide = ((length, features), F32)
     half = ((length, features), BF16)
     small = ((heads, length), F32)
+    turned = ((length, heads), F32)
     sent = ((17 * count, LANES), F32)
 
-    (fresh,) = staged(
-        fresh_kernel, 1 << 27, 60, dict(log=log, k=k, v=v), dict(out=sent),
-        [((length + 8, features), F32)],
-    )
+    (fresh,) = staged(fresh_kernel, 1 << 27, 60, (1, 2), dict(log=log, k=k, v=v), dict(out=sent))
     arrived = exchange(fresh, "seq")
-    cum, spread, grow, weight, inside = staged(
-        inside_kernel, 1 << 30, 60, dict(log=log, q=q, k=k, v=v),
-        dict(cum=small, spread=((length, heads * LANES), F32), grow=wide, weight=wide, inside=wide),
+    cum, cum_t, grow, weight, inside = staged(
+        inside_kernel, 1 << 30, 60, (2, 2), dict(log=log, q=q, k=k, v=v),
+        dict(cum=small, cum_t=turned, grow=turned, weight=turned, inside=wide),
     )
     arrived, inside = lax.optimization_barrier((arrived, inside))
     begun, decays = call(
         scan_kernel, [((16 * count, LANES), F32), ((count, LANES), F32)], 1 << 20, arrived
     )
     start = exchange(begun, "seq")
-    incoming, x = staged(
-        middle_kernel, 1 << 28, 60,
-        dict(gain=gain[None], q=q, g=g, state=start, grow=grow, inside=inside),
-        dict(out=sent, x=wide), [wide],
+    stats, incoming = staged(
+        middle_kernel, 1 << 28, 60, (2, 2),
+        dict(gain=gain[None], grow=grow, q=q, g=g, state=start, inside=inside),
+        dict(stats=turned, out=sent), [wide],
     )
     returned = exchange(incoming, "seq")
     z, d_queries, dk, dv = staged(
-        local_kernel, 1 << 31, 60,
-        dict(cum=cum, q=q, k=k, v=v, spread=spread, grow=grow, x=x, state=start),
+        local_kernel, 1 << 31, 60, (2, 2),
+        dict(
+            cum=cum, cum_t=cum_t, grow=grow, stats=stats, gain=gain[None],
+            q=q, k=k, v=v, g=g, state=start, inside=inside,
+        ),
         dict(z=small, dq=half, dk=wide, dv=wide),
     )
     returned, dk = lax.optimization_barrier((returned, dk))
@@ -452,8 +441,8 @@
     share = lax.all_to_all(share, "dp", 0, 0, tiled=True)
     (d_gain,) = call(gain_sum_kernel, [((pairs, LANES), F32)], 1 << 10, share)
     d_log, d_keys, d_values = staged(
-        last_kernel, 1 << 28, 60,
-        {"log": log, "z": z, "in": ended, "k": k, "v": v, "w": weight, "s": start, "dk": dk, "dv": dv},
+        last_kernel, 1 << 28, 60, (2, 2),
+        {"log": log, "z": z, "w": weight, "in": ended, "k": k, "v": v, "s": start, "dk": dk, "dv": dv},
         dict(log=small, dk=half, dv=half), [((heads, LANES), F32)],
     )
     return d_queries[None], d_keys[None], d_values[None], d_log[None], d_gain.reshape(features)

time: 132 us -> 132 us (level)
  Pallas kernels: 34.3 us -> 31.9 us
  blocking collectives: 47.1 us -> 48.5 us
  waiting for transfers between devices: 14.3 us -> 15.7 us
    pallas_call x5, Pallas kernels: 31.9 us -> 29.5 us  [staged(): pl.pallas_call(body, out_shape=results, in_specs=[hbm] * len(ins), out_sp...]
    all_to_all x2, blocking collectives: 47.1 us -> 48.5 us  [exchange(): return lax.all_to_all(pieces, axis, 0, 0, tiled=True).reshape(rows, lanes)]
  transfers between devices with their start and end apart: 3 -> 3, of which waited for: 3 -> 3; matrix products, arithmetic and copies ran while one was open for 0% -> 0% of each run, Pallas kernels for 18% -> 17%
where the time goes in v3:
time: 132 us; the launch traced here: 131 us
  blocking collectives  48.5 us (37%)
  starting transfers between devices  34.4 us (26%)
  Pallas kernels  31.9 us (24%)
  waiting for transfers between devices  15.7 us (12%)
    all_to_all x2, blocking collectives, exchange(): return lax.all_to_all(pieces, axis, 0, 0, tiled=True).reshape(rows, lanes)  48.5 us
    pallas_call x5, Pallas kernels, staged(): pl.pallas_call(body, out_shape=results, in_specs=[hbm] * len(ins), out_sp...  29.5 us
    all_to_all x2, starting transfers between devices, exchange(): return lax.all_to_all(pieces, axis, 0, 0, tiled=True).reshape(rows, lanes)  24.6 us
    all_to_all x2, waiting for transfers between devices, exchange(): return lax.all_to_all(pieces, axis, 0, 0, tiled=True).reshape(rows, lanes)  14.9 us
    all_to_all x1, starting transfers between devices, shards(): share = lax.all_to_all(share, 'dp', 0, 0, tiled=True)  9.77 us
  transfers between devices with their start and end apart: 3, of which 3 were waited for; matrix products, arithmetic and copies ran while one was open for 0% of the time, Pallas kernels for 17%

profile of v3, /device:TPU:1, one launch (start us, length us, event | category | flops | bytes accessed | tf_op | source)
XLA Modules:
  0.0 131.2 jit_solution(12396318060234078713)
XLA Ops:
  0.6 3.0 %shard_map.102 = f32[1088,128]{1,0:T(8,128)} custom-call(f32[32,128]{1,0:T(8,128)} %bitcast.43, bf16[128,2048]{1,0:T(8,128)(2,1)} %bitcast.29, bf16[128,2048]{1,0:T(8,128)(2,1)} %bitcast.33), custom_call_target="tpu_custom_call" | custom-call | flops 134217728 | bytes 1622016 | tf_op jit(solution)/shard_map/pallas_call | solution.py:369
  3.7 17.1 %all-to-all-start = ((f32[64,1,2176]{2,1,0:T(1,128)}), f32[64,1,2176]{2,1,0:T(1,128)S(1)}, u32[]{:S(2)}, u32[]{:S(2)}) async-start(f32[64,1,2176]{2,1,0:T(1,128)} %bitcast.28), calls=%async_computation | async-start | bytes 1114112 | tf_op jit(solution)/shard_map/all_to_all | solution.py:388
  20.8 5.1 %shard_map.101 = (f32[32,128]{1,0:T(8,128)}, f32[128,32]{1,0:T(8,128)}, f32[128,32]{1,0:T(8,128)}, f32[128,32]{1,0:T(8,128)}, f32[128,2048]{1,0:T(8,128)}) custom-call(f32[32,128]{1,0:T(8,128)} %bitcast.44, bf16[128,2048]{1,0:T(8,128)(2,1)} %bitcast.38, bf16[128,2048]{1,0:T(8,128)(2,1)} %bitcast.30, bf16[128,2048]{1,0:T(8,128)(2,1)} %bitcast.34), custom_call_target="tpu_custom_call" | custom-call | flops 1073741824 | bytes 2703360 | tf_op jit(solution)/shard_map/pallas_call | solution.py:369
  25.9 12.4 %all-to-all-done = f32[64,1,2176]{2,1,0:T(1,128)S(1)} async-done(((f32[64,1,2176]{2,1,0:T(1,128)}), f32[64,1,2176]{2,1,0:T(1,128)S(1)}, u32[]{:S(2)}, u32[]{:S(2)}) %all-to-all-start) | async-done | bytes 557088 | tf_op jit(solution)/shard_map/all_to_all | solution.py:388
  38.4 0.1 shard_map.103
  38.5 23.3 %all_to_all.25 = f32[64,1,2048]{2,1,0:T(1,128)} all-to-all(f32[64,1,2048]{2,1,0:T(1,128)S(1)} %bitcast.22), channel_id=1, replica_groups=mesh['dp'=8,'seq'=64] {'seq'}, dimensions={0} | all-to-all | bytes 1048576 | tf_op jit(solution)/shard_map/all_to_all | solution.py:388
  61.8 3.9 %shard_map.104 = (f32[128,32]{1,0:T(8,128)}, f32[1088,128]{1,0:T(8,128)}) custom-call(f32[1,2048]{1,0:T(1,128)} %bitcast.46, f32[128,32]{1,0:T(8,128)} %get-tuple-element.27.refs_1_.refs_2_, bf16[128,2048]{1,0:T(8,128)(2,1)} %bitcast.39, bf16[128,2048]{1,0:T(8,128)(2,1)} %bitcast.41, f32[1024,128]{1,0:T(8,128)} %bitcast.25, ...), custom_call_target="tpu_custom_call" | custom-call | flops 268435456 | bytes 3219456 | tf_op jit(solution)/shard_map/pallas_call | solution.py:369
  65.6 7.5 %all-to-all-start.2 = ((f32[64,1,2176]{2,1,0:T(1,128)}), f32[64,1,2176]{2,1,0:T(1,128)S(1)}, u32[]{:S(2)}, u32[]{:S(2)}) async-start(f32[64,1,2176]{2,1,0:T(1,128)} %bitcast.37), calls=%async_computation.2 | async-start | bytes 1114112 | tf_op jit(solution)/shard_map/all_to_all | solution.py:388
  73.1 13.5 %shard_map.105 = (f32[32,128]{1,0:T(8,128)}, bf16[128,2048]{1,0:T(8,128)(2,1)}, f32[128,2048]{1,0:T(8,128)}, f32[128,2048]{1,0:T(8,128)}) custom-call(f32[32,128]{1,0:T(8,128)} %get-tuple-element.25.refs_0_, f32[128,32]{1,0:T(8,128)} %get-tuple-element.26.refs_1_, f32[128,32]{1,0:T(8,128)} %get-tuple-element.27.refs_1_.refs_2_, ...), custom_call_target="tpu_custom_call" | custom-call | flops 2147483648 | bytes 6381568 | tf_op jit(solution)/shard_map/pallas_call | solution.py:369
  86.7 2.4 %all-to-all-done.2 = f32[64,1,2176]{2,1,0:T(1,128)S(1)} async-done(((f32[64,1,2176]{2,1,0:T(1,128)}), f32[64,1,2176]{2,1,0:T(1,128)S(1)}, u32[]{:S(2)}, u32[]{:S(2)}) %all-to-all-start.2) | async-done | bytes 557088 | tf_op jit(solution)/shard_map/all_to_all | solution.py:388
  89.1 0.1 shard_map.106
  89.3 25.2 %all_to_all.26 = f32[64,1,2176]{2,1,0:T(1,128)} all-to-all(f32[64,1,2176]{2,1,0:T(1,128)S(1)} %bitcast.21), channel_id=1, replica_groups=mesh['dp'=8,'seq'=64] {'seq'}, dimensions={0} | all-to-all | bytes 1114112 | tf_op jit(solution)/shard_map/all_to_all | solution.py:388
  114.5 1.5 %shard_map.108 = f32[8,16,128]{2,1,0:T(8,128)} custom-call(f32[1088,128]{1,0:T(8,128)} %bitcast.23), custom_call_target="tpu_custom_call" | custom-call | tf_op jit(solution)/shard_map/pallas_call | solution.py:433
  116.0 9.8 %all-to-all-start.4 = ((f32[8,16,128]{2,1,0:T(8,128)}), f32[8,16,128]{2,1,0:T(8,128)S(1)}, u32[]{:S(2)}, u32[]{:S(2)}) async-start(f32[8,16,128]{2,1,0:T(8,128)} %shard_map.108), calls=%async_computation.4 | async-start | bytes 131072 | tf_op jit(solution)/shard_map/all_to_all | solution.py:441
  125.8 4.0 %shard_map.107 = (f32[32,128]{1,0:T(8,128)}, bf16[128,2048]{1,0:T(8,128)(2,1)}, bf16[128,2048]{1,0:T(8,128)(2,1)}) custom-call(f32[32,128]{1,0:T(8,128)} %bitcast.45, f32[32,128]{1,0:T(8,128)} %get-tuple-element.34.refs_1_, f32[128,32]{1,0:T(8,128)} %get-tuple-element.35.refs_2_, f32[1088,128]{1,0:T(8,128)} %bitcast.24, bf16[128,2048]{1,0:T(8,128)(2,1)} %bitcast.32, ...), custom_call_target="tpu_custom_call" | custom-call | flops 268435456 | bytes 5341184 | tf_op jit(solution)/shard_map/pallas_call | solution.py:369
  129.8 0.9 all-to-all-done.4.in_ref
  130.6 0.6 shard_map.109
Async XLA Ops:
  3.7 34.7 %all-to-all-start = ((f32[64,1,2176]{2,1,0:T(1,128)}), f32[64,1,2176]{2,1,0:T(1,128)S(1)}, u32[]{:S(2)}, u32[]{:S(2)}) async-start(f32[64,1,2176]{2,1,0:T(1,128)} %bitcast.28), calls=%async_computation | async-start | bytes 1114112 | tf_op jit(solution)/shard_map/all_to_all | solution.py:388
  65.6 23.5 %all-to-all-start.2 = ((f32[64,1,2176]{2,1,0:T(1,128)}), f32[64,1,2176]{2,1,0:T(1,128)S(1)}, u32[]{:S(2)}, u32[]{:S(2)}) async-start(f32[64,1,2176]{2,1,0:T(1,128)} %bitcast.37), calls=%async_computation.2 | async-start | bytes 1114112 | tf_op jit(solution)/shard_map/all_to_all | solution.py:388
  116.0 14.6 %all-to-all-start.4 = ((f32[8,16,128]{2,1,0:T(8,128)}), f32[8,16,128]{2,1,0:T(8,128)S(1)}, u32[]{:S(2)}, u32[]{:S(2)}) async-start(f32[8,16,128]{2,1,0:T(8,128)} %shard_map.108), calls=%async_computation.4 | async-start | bytes 131072 | tf_op jit(solution)/shard_map/all_to_all | solution.py:441

commit v4 on v3

--- a/solution.py
+++ b/solution.py
@@ -126,18 +126,12 @@
         state = decay_ref[m : m + 1] * state + in_ref[17 * m : 17 * m + 16]
 
 
-def gain_kernel(in_ref, out_ref, rows, sems):
-    pairs = rows.shape[0]
-
-    def copy(p):
-        row = pl.ds(17 * 4 * p + 16, 1)
-        return pltpu.make_async_copy(in_ref.at[row, :], rows.at[pl.ds(p, 1), :], sems.at[p])
-
+def gain_kernel(in_ref, out_ref):
+    pairs = out_ref.shape[1]
     for p in range(pairs):
-        copy(p).start()
-    for p in range(pairs):
-        copy(p).wait()
-    out_ref[...] = jnp.broadcast_to(rows[...][None], out_ref.shape)
+        row = in_ref[17 * 4 * p + 16 : 17 * 4 * p + 17]
+        for d in range(out_ref.shape[0]):
+            out_ref[d, p : p + 1] = row
 
 
 def gain_sum_kernel(in_ref, out_ref):
@@ -148,7 +142,7 @@
 
 
 def inside_kernel(
-    ready, emit, log_ref, q_ref, k_ref, v_ref, cum_ref, cum_t_ref, grow_ref, weight_ref, inside_ref
+    ready, emit, log_ref, q_ref, k_ref, v_ref, cum_ref, cum_t_ref, weight_ref, inside_ref
 ):
     length, features = q_ref.shape
     ready("log")
@@ -157,7 +151,8 @@
     cum_ref[...] = exact(log, (row <= col).astype(F32))
     cumulative_t, total = sums(log, length)
     cum_t_ref[...] = cumulative_t
-    grow_ref[...] = jnp.exp(cumulative_t)
+    inside_ref[:, features : features + log.shape[0]] = jnp.exp(cumulative_t)
+    inside_ref[:, features + log.shape[0] :] = jnp.zeros((length, LANES - log.shape[0]), F32)
     weight_ref[...] = jnp.exp(total - cumulative_t)
     m0, m1 = side(LANES)
     for p in range(features // LANES):
@@ -170,29 +165,34 @@
         emit(p)
 
 
-def middle_kernel(
-    ready, emit, gain_ref, grow_ref, q_ref, g_ref, state_ref, inside_ref, stats_ref, out_ref, att
-):
+def growth_of(inside_ref, features):
+    return inside_ref[:, features : features + features // 64]
+
+
+def attend(ready, gain_ref, grow, q_ref, g_ref, state_ref, inside_ref, att):
     length, features = q_ref.shape
-    pairs = features // LANES
     m0, m1 = side(LANES)
     square = dot = jnp.zeros((length, LANES), F32)
-    ready("gain")
-    ready("grow")
-    grow = grow_ref[...]
-    for p in range(pairs):
+    for p in range(features // LANES):
         ready(p)
         lanes = pair(p)
-        carried = carry(q_ref[:, lanes], *block_diagonal(state_ref[64 * p : 64 * p + 64], m0, m1))
-        attended = inside_ref[:, lanes] + columns(grow, p) * carried
+        state = block_diagonal(state_ref[64 * p : 64 * p + 64], m0, m1)
+        attended = inside_ref[:, lanes] + columns(grow, p) * carry(q_ref[:, lanes], *state)
         att[:, lanes] = attended
         square = square + attended * attended
         dot = dot + attended * (gain_ref[:, lanes] * g_ref[:, lanes].astype(F32))
     scale = jnp.sqrt(jnp.sum(square, 1, keepdims=True) / features + EPSILON)
     inverse = 1.0 / scale
-    slope = jnp.sum(dot, 1, keepdims=True) * (inverse * inverse * inverse) / features
-    stats_ref[...] = jnp.where(iota(stats_ref.shape, 1) == 0, inverse, slope)
-    for p in range(pairs):
+    return inverse, jnp.sum(dot, 1, keepdims=True) * (inverse * inverse * inverse) / features
+
+
+def middle_kernel(
+    ready, emit, gain_ref, q_ref, g_ref, state_ref, inside_ref, out_ref, att
+):
+    features = q_ref.shape[1]
+    grow = growth_of(inside_ref, features)
+    inverse, slope = attend(ready, gain_ref, grow, q_ref, g_ref, state_ref, inside_ref, att)
+    for p in range(features // LANES):
         lanes = pair(p)
         attended = att[:, lanes]
         g = g_ref[:, lanes].astype(F32) * inverse
@@ -206,26 +206,26 @@
 
 
 def local_kernel(
-    ready, emit, cum_ref, cum_t_ref, grow_ref, stats_ref, gain_ref,
-    q_ref, k_ref, v_ref, g_ref, state_ref, inside_ref,
-    z_ref, dq_ref, dk_ref, dv_ref,
+    ready, emit, cum_ref, cum_t_ref, gain_ref, q_ref, k_ref, v_ref, g_ref, state_ref, inside_ref,
+    z_ref, dq_ref, dk_ref, dv_ref, att,
 ):
     length, features = q_ref.shape
     heads = cum_ref.shape[0]
     m0, m1 = side(LANES)
     row, col = iota((length, length), 0), iota((length, length), 1)
     z = jnp.zeros((heads, length), F32)
-    for name in ("cum", "cum_t", "grow", "stats", "gain"):
+    for name in ("cum", "cum_t", "gain", 0):
         ready(name)
-    cum_t, grow = cum_t_ref[...], grow_ref[...]
-    inverse, slope = stats_ref[:, 0:1], stats_ref[:, 1:2]
-    for p in range(features // LANES):
-        ready(p)
+    cum_t, grow = cum_t_ref[...], growth_of(inside_ref, features)
+    inverse, slope = attend(
+        lambda p: None, gain_ref, grow, q_ref, g_ref, state_ref, inside_ref, att
+    )
+    for p in range(features // LANES):
         lanes = pair(p)
         q, k, v = q_ref[:, lanes], k_ref[:, lanes], v_ref[:, lanes]
         state_hi, state_lo = block_diagonal(state_ref[64 * p : 64 * p + 64], m0, m1)
         growth = columns(grow, p)
-        attended = inside_ref[:, lanes] + growth * carry(q, state_hi, state_lo)
+        attended = att[:, lanes]
         g = g_ref[:, lanes].astype(F32) * inverse
         x = gain_ref[:, lanes] * g - attended * slope
         x_hi, x_lo = halves(x)
@@ -305,17 +305,18 @@
     )(*args)
 
 
-def staged(kernel, flops, limit, pieces, ins, outs, scratch=()):
+def staged(kernel, flops, limit, pieces, ins, outs, scratch=(), close=False):
     in_shapes = [(a.shape, a.dtype) for a in ins.values()]
     out_shapes = list(outs.values())
     names = [*ins, *outs]
     shapes = in_shapes + out_shapes
     small = [math.prod(shape) <= 4096 for shape, _ in shapes]
     count = len(shapes)
+    first = len(ins) if close else 0
 
     def body(*refs):
-        far, near = refs[:count], refs[count : 2 * count]
-        sems, own = refs[2 * count], refs[2 * count + 1 :]
+        far, near = refs[:count], refs[:first] + refs[count : 2 * count - first]
+        sems, own = refs[2 * count - first], refs[2 * count - first + 1 :]
 
         def copy(i, c):
             rows, lanes = shapes[i][0]
@@ -332,7 +333,7 @@
                 a, b = b, a
             return pltpu.make_async_copy(a, b, sems.at[i, c])
 
-        came = range(len(ins))
+        came = range(first, len(ins))
         sent = range(len(ins), count)
         steps = [PAIRS // cut for cut in pieces]
         for i in came:
@@ -369,10 +370,10 @@
     return pl.pallas_call(
         body,
         out_shape=results,
-        in_specs=[hbm] * len(ins),
+        in_specs=[pl.BlockSpec(memory_space=pltpu.VMEM) if close else hbm] * len(ins),
         out_specs=[hbm] * len(outs),
         scratch_shapes=[
-            *(pltpu.VMEM(shape, dtype) for shape, dtype in shapes),
+            *(pltpu.VMEM(shape, dtype) for shape, dtype in shapes[first:]),
             pltpu.SemaphoreType.DMA((count, max(pieces))),
             *(pltpu.VMEM(shape, dtype) for shape, dtype in scratch),
         ],
@@ -403,41 +404,34 @@
 
     (fresh,) = staged(fresh_kernel, 1 << 27, 60, (1, 2), dict(log=log, k=k, v=v), dict(out=sent))
     arrived = exchange(fresh, "seq")
-    cum, cum_t, grow, weight, inside = staged(
-        inside_kernel, 1 << 30, 60, (2, 2), dict(log=log, q=q, k=k, v=v),
-        dict(cum=small, cum_t=turned, grow=turned, weight=turned, inside=wide),
+    cum, cum_t, weight, inside = staged(
+        inside_kernel, 1 << 30, 60, (2, 1), dict(log=log, q=q, k=k, v=v),
+        dict(cum=small, cum_t=turned, weight=turned, inside=((length, features + LANES), F32)),
     )
     arrived, inside = lax.optimization_barrier((arrived, inside))
     begun, decays = call(
         scan_kernel, [((16 * count, LANES), F32), ((count, LANES), F32)], 1 << 20, arrived
     )
     start = exchange(begun, "seq")
-    stats, incoming = staged(
-        middle_kernel, 1 << 28, 60, (2, 2),
-        dict(gain=gain[None], grow=grow, q=q, g=g, state=start, inside=inside),
-        dict(stats=turned, out=sent), [wide],
+    (incoming,) = staged(
+        middle_kernel, 1 << 28, 8, (1, 2),
+        dict(gain=gain[None], q=q, g=g, state=start, inside=inside),
+        dict(out=sent), [wide], close=True,
     )
     returned = exchange(incoming, "seq")
     z, d_queries, dk, dv = staged(
-        local_kernel, 1 << 31, 60, (2, 2),
+        local_kernel, 1 << 31, 60, (1, 2),
         dict(
-            cum=cum, cum_t=cum_t, grow=grow, stats=stats, gain=gain[None],
+            cum=cum, cum_t=cum_t, gain=gain[None],
             q=q, k=k, v=v, g=g, state=start, inside=inside,
         ),
-        dict(z=small, dq=half, dk=wide, dv=wide),
+        dict(z=small, dq=half, dk=wide, dv=wide), [wide],
     )
     returned, dk = lax.optimization_barrier((returned, dk))
     (ended,) = call(back_kernel, [sent], 1 << 20, returned, decays)
     ended = exchange(ended, "seq")
-    shares = jax.ShapeDtypeStruct((lax.axis_size("dp"), pairs, LANES), F32)
-    share = pl.pallas_call(
-        gain_kernel,
-        out_shape=shares,
-        in_specs=[pl.BlockSpec(memory_space=pltpu.HBM)],
-        out_specs=pl.BlockSpec(memory_space=pltpu.VMEM),
-        scratch_shapes=[pltpu.VMEM((pairs, LANES), F32), pltpu.SemaphoreType.DMA((pairs,))],
-        compiler_params=pltpu.CompilerParams(vmem_limit_bytes=60 << 20),
-    )(ended)
+    shares = ((lax.axis_size("dp"), pairs, LANES), F32)
+    (share,) = call(gain_kernel, [shares], 1 << 10, ended)
     share = lax.all_to_all(share, "dp", 0, 0, tiled=True)
     (d_gain,) = call(gain_sum_kernel, [((pairs, LANES), F32)], 1 << 10, share)
     d_log, d_keys, d_values = staged(

time: 132 us -> 129 us (0.977)
  Pallas kernels: 31.9 us -> 29.5 us
    pallas_call x6 -> x5, Pallas kernels: 31 us -> 27.9 us  [staged(): pl.pallas_call(body, out_shape=results, in_specs=[pl.BlockSpec(memory_spa...]
  transfers between devices with their start and end apart: 3 -> 3, of which waited for: 3 -> 3; matrix products, arithmetic and copies ran while one was open for 0% -> 0% of each run, Pallas kernels for 17% -> 18%
where the time goes in v4:
time: 129 us; the launch traced here: 128 us
  blocking collectives  48 us (37%)
  starting transfers between devices  34.4 us (27%)
  Pallas kernels  29.5 us (23%)
  waiting for transfers between devices  15.8 us (12%)
    all_to_all x2, blocking collectives, exchange(): return lax.all_to_all(pieces, axis, 0, 0, tiled=True).reshape(rows, lanes)  48 us
    pallas_call x5, Pallas kernels, staged(): pl.pallas_call(body, out_shape=results, in_specs=[pl.BlockSpec(memory_spa...  27.9 us
    all_to_all x2, starting transfers between devices, exchange(): return lax.all_to_all(pieces, axis, 0, 0, tiled=True).reshape(rows, lanes)  24.6 us
    all_to_all x2, waiting for transfers between devices, exchange(): return lax.all_to_all(pieces, axis, 0, 0, tiled=True).reshape(rows, lanes)  14.9 us
    all_to_all x1, starting transfers between devices, shards(): share = lax.all_to_all(share, 'dp', 0, 0, tiled=True)  9.78 us
  transfers between devices with their start and end apart: 3, of which 3 were waited for; matrix products, arithmetic and copies ran while one was open for 0% of the time, Pallas kernels for 18%

profile of v4, /device:TPU:1, one launch (start us, length us, event | category | flops | bytes accessed | tf_op | source)
XLA Modules:
  0.0 128.5 jit_solution(16403427826591421558)
XLA Ops:
  0.6 3.0 %shard_map.102 = f32[1088,128]{1,0:T(8,128)} custom-call(f32[32,128]{1,0:T(8,128)} %bitcast.44, bf16[128,2048]{1,0:T(8,128)(2,1)} %bitcast.36, bf16[128,2048]{1,0:T(8,128)(2,1)} %bitcast.40), custom_call_target="tpu_custom_call" | custom-call | flops 134217728 | bytes 1622016 | tf_op jit(solution)/shard_map/pallas_call | solution.py:370
  3.6 17.1 %all-to-all-start = ((f32[64,1,2176]{2,1,0:T(1,128)}), f32[64,1,2176]{2,1,0:T(1,128)S(1)}, u32[]{:S(2)}, u32[]{:S(2)}) async-start(f32[64,1,2176]{2,1,0:T(1,128)} %bitcast.35), calls=%async_computation | async-start | bytes 1114112 | tf_op jit(solution)/shard_map/all_to_all | solution.py:389
  20.8 0.0 copy-start.3
  20.8 0.0 copy-start.4
  20.8 5.3 %shard_map.101 = (f32[32,128]{1,0:T(8,128)}, f32[128,32]{1,0:T(8,128)}, f32[128,32]{1,0:T(8,128)}, f32[128,2176]{1,0:T(8,128)}) custom-call(f32[32,128]{1,0:T(8,128)} %bitcast.45, bf16[128,2048]{1,0:T(8,128)(2,1)} %bitcast.27, bf16[128,2048]{1,0:T(8,128)(2,1)} %bitcast.37, bf16[128,2048]{1,0:T(8,128)(2,1)} %bitcast.41), custom_call_target="tpu_custom_call" | custom-call | flops 1073741824 | bytes 2752512 | tf_op jit(solution)/shard_map/pallas_call | solution.py:370
  26.2 0.0 copy-start.2
  26.2 0.0 copy-start.5
  26.2 12.2 %all-to-all-done = f32[64,1,2176]{2,1,0:T(1,128)S(1)} async-done(((f32[64,1,2176]{2,1,0:T(1,128)}), f32[64,1,2176]{2,1,0:T(1,128)S(1)}, u32[]{:S(2)}, u32[]{:S(2)}) %all-to-all-start) | async-done | bytes 557088 | tf_op jit(solution)/shard_map/all_to_all | solution.py:389
  38.3 0.1 shard_map.103
  38.5 23.2 %all_to_all.25 = f32[64,1,2048]{2,1,0:T(1,128)S(1)} all-to-all(f32[64,1,2048]{2,1,0:T(1,128)S(1)} %bitcast.32), channel_id=1, replica_groups=mesh['dp'=8,'seq'=64] {'seq'}, dimensions={0} | all-to-all | bytes 1048576 | tf_op jit(solution)/shard_map/all_to_all | solution.py:389
  61.6 0.0 copy-start.1
  61.6 0.0 copy-done.3
  61.6 0.0 copy-done.4
  61.7 0.0 copy-done.2
  61.7 0.0 copy-done.5
  61.7 2.4 %shard_map.105 = f32[1088,128]{1,0:T(8,128)} custom-call(f32[1,2048]{1,0:T(1,128)S(1)} %bitcast.34, bf16[128,2048]{1,0:T(8,128)(2,1)S(1)} %bitcast.29, bf16[128,2048]{1,0:T(8,128)(2,1)S(1)} %bitcast.31, f32[1024,128]{1,0:T(8,128)S(1)} %bitcast.21, f32[128,2176]{1,0:T(8,128)S(1)} %copy-done.2), custom_call_target="tpu_custom_call" | custom-call | flops 268435456 | bytes 3252224 | tf_op jit(solution)/shard_map/pallas_call | solution.py:370
  64.1 0.0 copy-done.1
  64.1 7.5 %all-to-all-start.2 = ((f32[64,1,2176]{2,1,0:T(1,128)}), f32[64,1,2176]{2,1,0:T(1,128)S(1)}, u32[]{:S(2)}, u32[]{:S(2)}) async-start(f32[64,1,2176]{2,1,0:T(1,128)} %bitcast.11), calls=%async_computation.2 | async-start | bytes 1114112 | tf_op jit(solution)/shard_map/all_to_all | solution.py:389
  71.6 13.2 %shard_map.104 = (f32[32,128]{1,0:T(8,128)}, bf16[128,2048]{1,0:T(8,128)(2,1)}, f32[128,2048]{1,0:T(8,128)}, f32[128,2048]{1,0:T(8,128)}) custom-call(f32[32,128]{1,0:T(8,128)} %get-tuple-element.22.refs_0_, f32[128,32]{1,0:T(8,128)} %get-tuple-element.23.refs_1_, f32[1,2048]{1,0:T(1,128)} %bitcast.33, bf16[128,2048]{1,0:T(8,128)(2,1)} %bitcast.28, ...), custom_call_target="tpu_custom_call" | custom-call | flops 2147483648 | bytes 6414336 | tf_op jit(solution)/shard_map/pallas_call | solution.py:370
  84.8 2.7 %all-to-all-done.2 = f32[64,1,2176]{2,1,0:T(1,128)S(1)} async-done(((f32[64,1,2176]{2,1,0:T(1,128)}), f32[64,1,2176]{2,1,0:T(1,128)S(1)}, u32[]{:S(2)}, u32[]{:S(2)}) %all-to-all-start.2) | async-done | bytes 557088 | tf_op jit(solution)/shard_map/all_to_all | solution.py:389
  87.6 0.1 shard_map.106
  87.7 24.8 %all_to_all.26 = f32[64,1,2176]{2,1,0:T(1,128)S(1)} all-to-all(f32[64,1,2176]{2,1,0:T(1,128)S(1)} %bitcast.26), channel_id=1, replica_groups=mesh['dp'=8,'seq'=64] {'seq'}, dimensions={0} | all-to-all | bytes 1114112 | tf_op jit(solution)/shard_map/all_to_all | solution.py:389
  112.5 0.0 copy-start
  112.5 0.7 shard_map.108
  113.2 9.8 %all-to-all-start.4 = ((f32[8,16,128]{2,1,0:T(8,128)}), f32[8,16,128]{2,1,0:T(8,128)S(1)}, u32[]{:S(2)}, u32[]{:S(2)}) async-start(f32[8,16,128]{2,1,0:T(8,128)} %shard_map.108), calls=%async_computation.4 | async-start | bytes 131072 | tf_op jit(solution)/shard_map/all_to_all | solution.py:435
  123.0 0.0 copy-done
  123.0 4.0 %shard_map.107 = (f32[32,128]{1,0:T(8,128)}, bf16[128,2048]{1,0:T(8,128)(2,1)}, bf16[128,2048]{1,0:T(8,128)(2,1)}) custom-call(f32[32,128]{1,0:T(8,128)} %bitcast.46, f32[32,128]{1,0:T(8,128)} %get-tuple-element.29.refs_1_, f32[128,32]{1,0:T(8,128)} %get-tuple-element.30.refs_2_, f32[1088,128]{1,0:T(8,128)} %bitcast.20, bf16[128,2048]{1,0:T(8,128)(2,1)} %bitcast.39, ...), custom_call_target="tpu_custom_call" | custom-call | flops 268435456 | bytes 5341184 | tf_op jit(solution)/shard_map/pallas_call | solution.py:370
  127.0 0.9 all-to-all-done.4.in_ref
  127.9 0.6 shard_map.109
Async XLA Ops:
  3.6 34.7 %all-to-all-start = ((f32[64,1,2176]{2,1,0:T(1,128)}), f32[64,1,2176]{2,1,0:T(1,128)S(1)}, u32[]{:S(2)}, u32[]{:S(2)}) async-start(f32[64,1,2176]{2,1,0:T(1,128)} %bitcast.35), calls=%async_computation | async-start | bytes 1114112 | tf_op jit(solution)/shard_map/all_to_all | solution.py:389
  20.8 40.9 %copy-start.3 = (bf16[1,128,2048]{2,1,0:T(8,128)(2,1)S(1)}, bf16[1,128,2048]{2,1,0:T(8,128)(2,1)}, u32[]{:S(2)}) copy-start(bf16[1,128,2048]{2,1,0:T(8,128)(2,1)} %param.6) | copy-start | bytes 1572868
  20.8 40.9 %copy-start.4 = (bf16[1,128,2048]{2,1,0:T(8,128)(2,1)S(1)}, bf16[1,128,2048]{2,1,0:T(8,128)(2,1)}, u32[]{:S(2)}) copy-start(bf16[1,128,2048]{2,1,0:T(8,128)(2,1)} %param.11) | copy-start | bytes 1572868
  26.2 35.5 %copy-start.2 = (f32[128,2176]{1,0:T(8,128)S(1)}, f32[128,2176]{1,0:T(8,128)}, u32[]{:S(2)}) copy-start(f32[128,2176]{1,0:T(8,128)} %get-tuple-element.27.refs_8_.refs_4_) | copy-start | bytes 3342340
  26.2 35.5 %copy-start.5 = (f32[2048]{0:T(1024)S(1)}, f32[2048]{0:T(1024)}, u32[]{:S(2)}) copy-start(f32[2048]{0:T(1024)} %param.10) | copy-start | bytes 24580
  61.6 2.4 %copy-start.1 = (f32[64,1,2048]{2,1,0:T(1,128)}, f32[64,1,2048]{2,1,0:T(1,128)S(1)}, u32[]{:S(2)}) copy-start(f32[64,1,2048]{2,1,0:T(1,128)S(1)} %all_to_all.25) | copy-start | bytes 1572868
  64.1 23.5 %all-to-all-start.2 = ((f32[64,1,2176]{2,1,0:T(1,128)}), f32[64,1,2176]{2,1,0:T(1,128)S(1)}, u32[]{:S(2)}, u32[]{:S(2)}) async-start(f32[64,1,2176]{2,1,0:T(1,128)} %bitcast.11), calls=%async_computation.2 | async-start | bytes 1114112 | tf_op jit(solution)/shard_map/all_to_all | solution.py:389
  112.5 10.5 %copy-start = (f32[64,1,2176]{2,1,0:T(1,128)}, f32[64,1,2176]{2,1,0:T(1,128)S(1)}, u32[]{:S(2)}) copy-start(f32[64,1,2176]{2,1,0:T(1,128)S(1)} %all_to_all.26) | copy-start | bytes 1671172
  113.2 14.6 %all-to-all-start.4 = ((f32[8,16,128]{2,1,0:T(8,128)}), f32[8,16,128]{2,1,0:T(8,128)S(1)}, u32[]{:S(2)}, u32[]{:S(2)}) async-start(f32[8,16,128]{2,1,0:T(8,128)} %shard_map.108), calls=%async_computation.4 | async-start | bytes 131072 | tf_op jit(solution)/shard_map/all_to_all | solution.py:435

commit v5 on v4

--- a/solution.py
+++ b/solution.py
@@ -87,6 +87,15 @@
         j = 17 * (4 * p + i)
         out_ref[j : j + 16] = state[16 * i : 16 * i + 16]
         out_ref[j + 16 : j + 17] = row
+
+
+def tied(product, moves_t, moves, p, keep):
+    parts = []
+    for a in range(2):
+        h = 2 * p + a
+        same = keep & (moves_t[:, h : h + 1] == moves[h : h + 1, :])
+        parts.append(jnp.sum(jnp.where(same, product[:, pair(a)], 0.0), 0, keepdims=True))
+    return jnp.concatenate(parts, 1)
 
 
 def fresh_kernel(ready, emit, log_ref, k_ref, v_ref, out_ref):
@@ -206,17 +215,21 @@
 
 
 def local_kernel(
-    ready, emit, cum_ref, cum_t_ref, gain_ref, q_ref, k_ref, v_ref, g_ref, state_ref, inside_ref,
-    z_ref, dq_ref, dk_ref, dv_ref, att,
+    ready, emit, log_ref, cum_ref, cum_t_ref, gain_ref,
+    q_ref, k_ref, v_ref, g_ref, state_ref, inside_ref,
+    z_ref, dq_ref, dk_ref, dv_ref, att, ties,
 ):
     length, features = q_ref.shape
     heads = cum_ref.shape[0]
     m0, m1 = side(LANES)
     row, col = iota((length, length), 0), iota((length, length), 1)
     z = jnp.zeros((heads, length), F32)
-    for name in ("cum", "cum_t", "gain", 0):
+    for name in ("log", "cum", "cum_t", "gain", 0):
         ready(name)
     cum_t, grow = cum_t_ref[...], growth_of(inside_ref, features)
+    moved = (log_ref[...] != 0.0).astype(F32).astype(BF16)
+    moves = mm(moved, (row <= col).astype(F32).astype(BF16))
+    moves_t = mm((row >= col).astype(F32).astype(BF16), moved, NT)
     inverse, slope = attend(
         lambda p: None, gain_ref, grow, q_ref, g_ref, state_ref, inside_ref, att
     )
@@ -233,21 +246,28 @@
         k2, q2, v2 = stacked(k, m0, m1), stacked(q, m0, m1), stacked(v, m0, m1)
         x2_hi, x2_lo = stacked(x_hi, m0, m1), stacked(x_lo, m0, m1)
         d_weight = mm(jnp.concatenate([x_hi, x_lo], 1), jnp.concatenate([v2, v2], 1), NT)
-        hi, lo = halves(d_weight * decay_pair(cum_t, cum_ref, p, row >= col, 1.0))
+        d_score = d_weight * decay_pair(cum_t, cum_ref, p, row >= col, 1.0)
+        down = tied(d_score * mm(q, k2, NT), moves_t, moves, p, row >= col)
+        hi, lo = halves(d_score)
         dq = mm(hi, k2) + mm(lo, k2) + mm(y_hi, state_lo, NT)
         dq = dq + mm(jnp.concatenate([y_hi, y_lo], 1), jnp.concatenate([state_hi, state_hi], 1), NT)
         dq_ref[:, lanes] = dq.astype(BF16)
         decay = decay_pair(cum_t, cum_ref, p, row <= col, -1.0)
-        hi, lo = halves(mm(k, q2, NT) * decay)
+        score = mm(k, q2, NT)
+        hi, lo = halves(score * decay)
         dv_ref[:, lanes] = mm(hi, x2_hi) + mm(lo, x2_hi) + mm(hi, x2_lo)
         d_weight = mm(jnp.concatenate([v, v], 1), jnp.concatenate([x2_hi, x2_lo], 1), NT)
-        hi, lo = halves(d_weight * decay)
+        d_score = d_weight * decay
+        across = tied(d_score * score, moves_t, moves, p, row <= col)
+        for a in range(2):
+            ties[2 * p + a : 2 * p + a + 1] = 0.5 * (down - across)[:, pair(a)]
+        hi, lo = halves(d_score)
         dk = mm(hi, q2) + mm(lo, q2)
         dk_ref[:, lanes] = dk
         hi, lo = halves(q.astype(F32) * dq - k.astype(F32) * dk)
         z = z + mm(picker(heads, p), jnp.concatenate([hi, lo], 1), NT)
         emit(p)
-    z_ref[...] = exact(z, (row >= col).astype(F32))
+    z_ref[...] = exact(z + ties[...], (row >= col).astype(F32))
 
 
 def picker(heads, p):
@@ -422,10 +442,10 @@
     z, d_queries, dk, dv = staged(
         local_kernel, 1 << 31, 60, (1, 2),
         dict(
-            cum=cum, cum_t=cum_t, gain=gain[None],
+            log=log, cum=cum, cum_t=cum_t, gain=gain[None],
             q=q, k=k, v=v, g=g, state=start, inside=inside,
         ),
-        dict(z=small, dq=half, dk=wide, dv=wide), [wide],
+        dict(z=small, dq=half, dk=wide, dv=wide), [wide, small],
     )
     returned, dk = lax.optimization_barrier((returned, dk))
     (ended,) = call(back_kernel, [sent], 1 << 20, returned, decays)

time: 129 us -> 131 us (1.016)
  waiting for transfers between devices: 15.8 us -> 13.6 us
  Pallas kernels: 29.5 us -> 31.7 us
  blocking collectives: 48 us -> 50.1 us
    all_to_all x2, blocking collectives: 48 us -> 50.1 us  [exchange(): return lax.all_to_all(pieces, axis, 0, 0, tiled=True).reshape(rows, lanes)]
    pallas_call x5, Pallas kernels: 27.9 us -> 30.1 us  [staged(): pl.pallas_call(body, out_shape=results, in_specs=[pl.BlockSpec(memory_spa...]
    all_to_all x2, waiting for transfers between devices: 14.9 us -> 12.8 us  [exchange(): return lax.all_to_all(pieces, axis, 0, 0, tiled=True).reshape(rows, lanes)]
  transfers between devices with their start and end apart: 3 -> 3, of which waited for: 3 -> 3; matrix products, arithmetic and copies ran while one was open for 0% -> 0% of each run, Pallas kernels for 18% -> 19%
where the time goes in v5:
time: 131 us
  blocking collectives  50.1 us (38%)
  starting transfers between devices  34.4 us (26%)
  Pallas kernels  31.7 us (24%)
  waiting for transfers between devices  13.6 us (10%)
    all_to_all x2, blocking collectives, exchange(): return lax.all_to_all(pieces, axis, 0, 0, tiled=True).reshape(rows, lanes)  50.1 us
    pallas_call x5, Pallas kernels, staged(): pl.pallas_call(body, out_shape=results, in_specs=[pl.BlockSpec(memory_spa...  30.1 us
    all_to_all x2, starting transfers between devices, exchange(): return lax.all_to_all(pieces, axis, 0, 0, tiled=True).reshape(rows, lanes)  24.6 us
    all_to_all x2, waiting for transfers between devices, exchange(): return lax.all_to_all(pieces, axis, 0, 0, tiled=True).reshape(rows, lanes)  12.8 us
    all_to_all x1, starting transfers between devices, shards(): share = lax.all_to_all(share, 'dp', 0, 0, tiled=True)  9.78 us
  transfers between devices with their start and end apart: 3, of which 3 were waited for; matrix products, arithmetic and copies ran while one was open for 0% of the time, Pallas kernels for 19%

profile of v5, /device:TPU:1, one launch (start us, length us, event | category | flops | bytes accessed | tf_op | source)
XLA Modules:
  0.0 130.6 jit_solution(17152070622744692677)
XLA Ops:
  0.6 3.0 %shard_map.102 = f32[1088,128]{1,0:T(8,128)} custom-call(f32[32,128]{1,0:T(8,128)} %bitcast.44, bf16[128,2048]{1,0:T(8,128)(2,1)} %bitcast.36, bf16[128,2048]{1,0:T(8,128)(2,1)} %bitcast.40), custom_call_target="tpu_custom_call" | custom-call | flops 134217728 | bytes 1622016 | tf_op jit(solution)/shard_map/pallas_call | solution.py:390
  3.6 17.1 %all-to-all-start = ((f32[64,1,2176]{2,1,0:T(1,128)}), f32[64,1,2176]{2,1,0:T(1,128)S(1)}, u32[]{:S(2)}, u32[]{:S(2)}) async-start(f32[64,1,2176]{2,1,0:T(1,128)} %bitcast.35), calls=%async_computation | async-start | bytes 1114112 | tf_op jit(solution)/shard_map/all_to_all | solution.py:409
  20.8 0.0 copy-start.3
  20.8 0.0 copy-start.4
  20.8 5.3 %shard_map.101 = (f32[32,128]{1,0:T(8,128)}, f32[128,32]{1,0:T(8,128)}, f32[128,32]{1,0:T(8,128)}, f32[128,2176]{1,0:T(8,128)}) custom-call(f32[32,128]{1,0:T(8,128)} %bitcast.45, bf16[128,2048]{1,0:T(8,128)(2,1)} %bitcast.27, bf16[128,2048]{1,0:T(8,128)(2,1)} %bitcast.37, bf16[128,2048]{1,0:T(8,128)(2,1)} %bitcast.41), custom_call_target="tpu_custom_call" | custom-call | flops 1073741824 | bytes 2752512 | tf_op jit(solution)/shard_map/pallas_call | solution.py:390
  26.2 0.0 copy-start.2
  26.2 0.0 copy-start.5
  26.2 12.2 %all-to-all-done = f32[64,1,2176]{2,1,0:T(1,128)S(1)} async-done(((f32[64,1,2176]{2,1,0:T(1,128)}), f32[64,1,2176]{2,1,0:T(1,128)S(1)}, u32[]{:S(2)}, u32[]{:S(2)}) %all-to-all-start) | async-done | bytes 557088 | tf_op jit(solution)/shard_map/all_to_all | solution.py:409
  38.3 0.1 shard_map.103
  38.5 23.2 %all_to_all.25 = f32[64,1,2048]{2,1,0:T(1,128)S(1)} all-to-all(f32[64,1,2048]{2,1,0:T(1,128)S(1)} %bitcast.32), channel_id=1, replica_groups=mesh['dp'=8,'seq'=64] {'seq'}, dimensions={0} | all-to-all | bytes 1048576 | tf_op jit(solution)/shard_map/all_to_all | solution.py:409
  61.6 0.0 copy-start.1
  61.6 0.0 copy-done.3
  61.7 0.0 copy-done.4
  61.7 0.0 copy-done.2
  61.7 0.0 copy-done.5
  61.7 2.4 %shard_map.105 = f32[1088,128]{1,0:T(8,128)} custom-call(f32[1,2048]{1,0:T(1,128)S(1)} %bitcast.34, bf16[128,2048]{1,0:T(8,128)(2,1)S(1)} %bitcast.29, bf16[128,2048]{1,0:T(8,128)(2,1)S(1)} %bitcast.31, f32[1024,128]{1,0:T(8,128)S(1)} %bitcast.21, f32[128,2176]{1,0:T(8,128)S(1)} %copy-done.2), custom_call_target="tpu_custom_call" | custom-call | flops 268435456 | bytes 3252224 | tf_op jit(solution)/shard_map/pallas_call | solution.py:390
  64.1 0.0 copy-done.1
  64.1 7.5 %all-to-all-start.2 = ((f32[64,1,2176]{2,1,0:T(1,128)}), f32[64,1,2176]{2,1,0:T(1,128)S(1)}, u32[]{:S(2)}, u32[]{:S(2)}) async-start(f32[64,1,2176]{2,1,0:T(1,128)} %bitcast.11), calls=%async_computation.2 | async-start | bytes 1114112 | tf_op jit(solution)/shard_map/all_to_all | solution.py:409
  71.6 15.4 %shard_map.104 = (f32[32,128]{1,0:T(8,128)}, bf16[128,2048]{1,0:T(8,128)(2,1)}, f32[128,2048]{1,0:T(8,128)}, f32[128,2048]{1,0:T(8,128)}) custom-call(f32[32,128]{1,0:T(8,128)} %bitcast.46, f32[32,128]{1,0:T(8,128)} %get-tuple-element.22.refs_1_, f32[128,32]{1,0:T(8,128)} %get-tuple-element.23.refs_2_, f32[1,2048]{1,0:T(1,128)} %bitcast.33, ...), custom_call_target="tpu_custom_call" | custom-call | flops 2147483648 | bytes 6430720 | tf_op jit(solution)/shard_map/pallas_call | solution.py:390
  87.0 0.6 all-to-all-done.2
  87.6 0.1 shard_map.106
  87.7 26.9 %all_to_all.26 = f32[64,1,2176]{2,1,0:T(1,128)S(1)} all-to-all(f32[64,1,2176]{2,1,0:T(1,128)S(1)} %bitcast.26), channel_id=1, replica_groups=mesh['dp'=8,'seq'=64] {'seq'}, dimensions={0} | all-to-all | bytes 1114112 | tf_op jit(solution)/shard_map/all_to_all | solution.py:409
  114.7 0.0 copy-start
  114.7 0.7 shard_map.108
  115.4 9.8 %all-to-all-start.4 = ((f32[8,16,128]{2,1,0:T(8,128)}), f32[8,16,128]{2,1,0:T(8,128)S(1)}, u32[]{:S(2)}, u32[]{:S(2)}) async-start(f32[8,16,128]{2,1,0:T(8,128)} %shard_map.108), calls=%async_computation.4 | async-start | bytes 131072 | tf_op jit(solution)/shard_map/all_to_all | solution.py:455
  125.1 0.0 copy-done
  125.1 4.0 %shard_map.107 = (f32[32,128]{1,0:T(8,128)}, bf16[128,2048]{1,0:T(8,128)(2,1)}, bf16[128,2048]{1,0:T(8,128)(2,1)}) custom-call(f32[32,128]{1,0:T(8,128)} %bitcast.47, f32[32,128]{1,0:T(8,128)} %get-tuple-element.29.refs_1_, f32[128,32]{1,0:T(8,128)} %get-tuple-element.30.refs_2_, f32[1088,128]{1,0:T(8,128)} %bitcast.20, bf16[128,2048]{1,0:T(8,128)(2,1)} %bitcast.39, ...), custom_call_target="tpu_custom_call" | custom-call | flops 268435456 | bytes 5341184 | tf_op jit(solution)/shard_map/pallas_call | solution.py:390
  129.1 0.9 all-to-all-done.4.in_ref
  130.0 0.6 shard_map.109
Async XLA Ops:
  3.6 34.7 %all-to-all-start = ((f32[64,1,2176]{2,1,0:T(1,128)}), f32[64,1,2176]{2,1,0:T(1,128)S(1)}, u32[]{:S(2)}, u32[]{:S(2)}) async-start(f32[64,1,2176]{2,1,0:T(1,128)} %bitcast.35), calls=%async_computation | async-start | bytes 1114112 | tf_op jit(solution)/shard_map/all_to_all | solution.py:409
  20.8 40.9 %copy-start.3 = (bf16[1,128,2048]{2,1,0:T(8,128)(2,1)S(1)}, bf16[1,128,2048]{2,1,0:T(8,128)(2,1)}, u32[]{:S(2)}) copy-start(bf16[1,128,2048]{2,1,0:T(8,128)(2,1)} %param.6) | copy-start | bytes 1572868
  20.8 40.9 %copy-start.4 = (bf16[1,128,2048]{2,1,0:T(8,128)(2,1)S(1)}, bf16[1,128,2048]{2,1,0:T(8,128)(2,1)}, u32[]{:S(2)}) copy-start(bf16[1,128,2048]{2,1,0:T(8,128)(2,1)} %param.11) | copy-start | bytes 1572868
  26.2 35.5 %copy-start.2 = (f32[128,2176]{1,0:T(8,128)S(1)}, f32[128,2176]{1,0:T(8,128)}, u32[]{:S(2)}) copy-start(f32[128,2176]{1,0:T(8,128)} %get-tuple-element.27.refs_9_.refs_4_) | copy-start | bytes 3342340
  26.2 35.5 %copy-start.5 = (f32[2048]{0:T(1024)S(1)}, f32[2048]{0:T(1024)}, u32[]{:S(2)}) copy-start(f32[2048]{0:T(1024)} %param.10) | copy-start | bytes 24580
  61.6 2.4 %copy-start.1 = (f32[64,1,2048]{2,1,0:T(1,128)}, f32[64,1,2048]{2,1,0:T(1,128)S(1)}, u32[]{:S(2)}) copy-start(f32[64,1,2048]{2,1,0:T(1,128)S(1)} %all_to_all.25) | copy-start | bytes 1572868
  64.1 23.5 %all-to-all-start.2 = ((f32[64,1,2176]{2,1,0:T(1,128)}), f32[64,1,2176]{2,1,0:T(1,128)S(1)}, u32[]{:S(2)}, u32[]{:S(2)}) async-start(f32[64,1,2176]{2,1,0:T(1,128)} %bitcast.11), calls=%async_computation.2 | async-start | bytes 1114112 | tf_op jit(solution)/shard_map/all_to_all | solution.py:409
  114.7 10.5 %copy-start = (f32[64,1,2176]{2,1,0:T(1,128)}, f32[64,1,2176]{2,1,0:T(1,128)S(1)}, u32[]{:S(2)}) copy-start(f32[64,1,2176]{2,1,0:T(1,128)S(1)} %all_to_all.26) | copy-start | bytes 1671172
  115.4 14.6 %all-to-all-start.4 = ((f32[8,16,128]{2,1,0:T(8,128)}), f32[8,16,128]{2,1,0:T(8,128)S(1)}, u32[]{:S(2)}, u32[]{:S(2)}) async-start(f32[8,16,128]{2,1,0:T(8,128)} %shard_map.108), calls=%async_computation.4 | async-start | bytes 131072 | tf_op jit(solution)/shard_map/all_to_all | solution.py:455
